TPU v7x, 32 devices: a whole 2x2x4 slice. The times are simulated.
32 devices in a mesh: parts: 2 (over y), seq: 8 (over z, core), rep: 2 (over x), head: 1.
Axes of the slice: x: 2, y: 2, z: 4, core: 2. Of those that a mesh axis runs over, the one named last changes fastest.
Arguments:
- activations: bfloat16 [4, 1024, 2048], P(('parts', 'rep'), 'seq', 'head'), parts along dimension 0, may hold values from -6 to 6
- value_weight: bfloat16 [2048, 2048], P(('seq', 'rep'), 'head'), may hold values from -0.125 to 0.125
- query_in: bfloat16 [4, 1024, 2048], P(('parts', 'rep'), 'seq', 'head'), parts along dimension 0, may hold values from -6 to 6
- key_in: bfloat16 [4, 1024, 2048], P(('parts', 'rep'), 'seq', 'head'), parts along dimension 0, may hold values from -6 to 6
- grad_out: bfloat16 [4, 1024, 2048], P(('parts', 'rep'), 'seq', 'head'), parts along dimension 0, may hold values from -6 to 6
- conv_kernel: float32 [3, 4, 2048], P(None, None, 'head'), may hold values from -3 to 3
- log_gate: float32 [4, 16, 1024], P(('parts', 'rep'), 'head', 'seq'), parts along dimension 0, as said below
Outputs:
- attn_out: bfloat16 [4, 1024, 2048], P(('parts', 'rep'), 'seq', 'head'), parts along dimension 0
- grad_query: bfloat16 [4, 1024, 2048], P(('parts', 'rep'), 'seq', 'head'), parts along dimension 0
- grad_key: bfloat16 [4, 1024, 2048], P(('parts', 'rep'), 'seq', 'head'), parts along dimension 0
- grad_x: bfloat16 [4, 1024, 2048], P(('parts', 'rep'), 'seq', 'head'), parts along dimension 0
- grad_w: float32 [4096, 2048], P(('parts', 'seq', 'rep'), 'head'), parts along dimension 0
- grad_conv: float32 [6, 4, 2048], P('parts', None, 'head'), parts along dimension 0
There are 2 independent parts, one for each index of `parts`. A program takes and returns all parts, laid end to end along the dimension named above; an argument that names none is the same for every part. Nothing has to cross between parts.
Inputs may be any that keep to these rules, and one draw needn't show every extreme that they name: `log_gate`: every entry is below zero.
All inputs are finite; a program needn't handle non-finite values.
Results may differ from a plain program's by a relative error of at most 0.015.
Values may be sent and summed in bfloat16 or wider, within the bound.
A program may use at most 128 MiB of HBM per device.

v0:
```python
import math

import jax
import jax.numpy as jnp
from jax import lax
from jax.sharding import PartitionSpec as P

EPSILON = 1e-06


def shifted(block, axis, distance):
    devices = range(lax.axis_size(axis))
    route = [(i - distance, i) for i in devices if i - distance in devices]
    return lax.ppermute(block, axis, route)


def prefix(part, axis, combine, identity, reverse):
    count = lax.axis_size(axis)
    place = lax.axis_index(axis)
    ahead = count - 1 - place if reverse else place
    gathered = jax.tree.map(lambda a: lax.all_gather(a, axis), part)
    state = jax.tree.map(lambda a, e: jnp.zeros_like(a) + jnp.asarray(e, a.dtype), part, identity)

    def one(step, state):
        source = count - 1 - step if reverse else step
        return combine(
            state, jax.tree.map(lambda a: lax.dynamic_index_in_dim(a, source, 0, False), gathered)
        )

    return lax.fori_loop(0, ahead, one, state)


def carried_in(value, axis, combine, identity, reverse):
    length, mine = (lax.axis_size(axis), lax.axis_index(axis))
    everything = jax.tree.map(
        lambda part, kind: lax.all_gather(part.astype(kind), axis),
        value,
        (jnp.bfloat16, jnp.bfloat16),
    )
    start = jax.tree.map(
        lambda part, zero: jnp.broadcast_to(jnp.asarray(zero, part.dtype), part.shape),
        value,
        identity,
    )

    def step(k, before):
        at = length - 1 - k if reverse else k
        reached = at > mine if reverse else at < mine
        new = combine(
            before, jax.tree.map(lambda part, own: part[at].astype(own.dtype), everything, value)
        )
        return jax.tree.map(lambda a, b: jnp.where(reached, a, b), new, before)

    return lax.fori_loop(0, length, step, start)


def chain_join(earlier, following):
    return (earlier[0] * following[0], following[0][:, None, None] * earlier[1] + following[1])


def causal_filter(stream_rows, previous, kernel_taps):
    rim_rows = previous.shape[0]
    length = stream_rows.shape[0]
    extended = jnp.concatenate([previous, stream_rows], axis=0).astype(jnp.float32)
    result = jnp.zeros(stream_rows.shape, jnp.float32)
    for offset in range(kernel_taps.shape[0]):
        result = (
            result + kernel_taps[offset] * extended[rim_rows - offset : rim_rows - offset + length]
        )
    return result


def filter_back(post_rows, following_rows, kernel_taps):
    length = post_rows.shape[0]
    extended = jnp.concatenate([post_rows, following_rows], axis=0)
    result = jnp.zeros(post_rows.shape, jnp.float32)
    for offset in range(kernel_taps.shape[0]):
        result = result + kernel_taps[offset] * extended[offset : offset + length]
    return result


def tap_sums(post_rows, stream_rows, previous, kernel_width):
    rim_rows = previous.shape[0]
    length = stream_rows.shape[0]
    extended = jnp.concatenate([previous, stream_rows], axis=0).astype(jnp.float32)
    return jnp.stack(
        [
            jnp.sum(post_rows * extended[rim_rows - offset : rim_rows - offset + length], axis=0)
            for offset in range(kernel_width)
        ]
    )


def local(activations, value_weight, query_in, key_in, grad_out, conv_kernel, log_gate):
    tok_rows = query_in.shape[1]
    channels = query_in.shape[2]
    head_count = log_gate.shape[1]
    head_size = channels // head_count
    kernel_width = conv_kernel.shape[1]
    rim_rows = kernel_width - 1
    grad_scale = 1.0 / math.sqrt(lax.axis_size("seq") * lax.axis_size("rep") * tok_rows)
    query_rows = query_in[0]
    key_rows = key_in[0]
    gathered = lax.all_gather(activations, "head", axis=2, tiled=True)[0]
    columns = gathered
    value_f32 = jnp.dot(
        columns,
        lax.all_gather(value_weight, ("seq", "rep"), axis=0, tiled=True),
        preferred_element_type=jnp.float32,
    )
    value_raw = value_f32.astype(jnp.bfloat16)
    before_all = shifted(
        jnp.stack(
            [
                query_rows[tok_rows - rim_rows :],
                key_rows[tok_rows - rim_rows :],
                value_raw[tok_rows - rim_rows :],
            ]
        ),
        "seq",
        1,
    )
    before = (before_all[0], before_all[1], before_all[2])
    raw_rows = (query_rows, key_rows, value_raw)
    convolved = [
        causal_filter(raw_rows[which], before[which], conv_kernel[which]).astype(jnp.bfloat16)
        for which in range(3)
    ]
    query_heads = convolved[0].reshape(tok_rows, head_count, head_size)
    key_heads = convolved[1].reshape(tok_rows, head_count, head_size)
    value_heads = convolved[2].reshape(tok_rows, head_count, head_size)
    cumulative = jnp.cumsum(log_gate[0], axis=1)
    final_cum = cumulative[:, -1]
    block_decay = jnp.exp(final_cum)
    rising = jnp.exp(cumulative).T[:, :, None]
    shrink = jnp.exp(final_cum[:, None] - cumulative).T[:, :, None]
    mixing = jnp.exp(-jnp.abs(cumulative[:, :, None] - cumulative[:, None, :]))
    scores = (
        mixing
        * jnp.einsum("thd,shd->hts", query_heads, key_heads, preferred_element_type=jnp.float32)
    ).astype(jnp.bfloat16)
    fwd_sum = jnp.einsum(
        "thd,the->hde",
        (shrink * key_heads).astype(jnp.bfloat16),
        value_heads,
        preferred_element_type=jnp.float32,
    )
    back_sum = jnp.einsum(
        "thd,the->hde",
        (rising * key_heads).astype(jnp.bfloat16),
        value_heads,
        preferred_element_type=jnp.float32,
    )
    identity = (
        jnp.ones((head_count,), jnp.float32),
        jnp.zeros((head_count, head_size, head_size), jnp.float32),
    )
    left_b = prefix((block_decay, fwd_sum), "seq", chain_join, identity, False)[1].astype(
        jnp.bfloat16
    )
    right_b = prefix((block_decay, back_sum), "seq", chain_join, identity, True)[1].astype(
        jnp.bfloat16
    )
    attn = rising * jnp.einsum(
        "thd,hde->the", query_heads, left_b, preferred_element_type=jnp.float32
    )
    attn = attn + shrink * jnp.einsum(
        "thd,hde->the", query_heads, right_b, preferred_element_type=jnp.float32
    )
    attn = attn + jnp.einsum(
        "hts,she->the", scores, value_heads, preferred_element_type=jnp.float32
    )
    root_mean = jnp.sqrt(jnp.mean(attn * attn, axis=2, keepdims=True) + EPSILON)
    normed = attn / root_mean
    attn_out = normed.astype(jnp.bfloat16).reshape(1, tok_rows, channels)
    upstream = grad_out[0].reshape(tok_rows, head_count, head_size).astype(jnp.float32)
    grad_attn = (
        (upstream - normed * jnp.mean(upstream * normed, axis=2, keepdims=True)) / root_mean
    ).astype(jnp.bfloat16)
    grad_scores = (
        mixing
        * jnp.einsum("the,she->hts", grad_attn, value_heads, preferred_element_type=jnp.float32)
    ).astype(jnp.bfloat16)
    fwd_grad = jnp.einsum(
        "thd,the->hde",
        (shrink * query_heads).astype(jnp.bfloat16),
        grad_attn,
        preferred_element_type=jnp.float32,
    )
    back_grad = jnp.einsum(
        "thd,the->hde",
        (rising * query_heads).astype(jnp.bfloat16),
        grad_attn,
        preferred_element_type=jnp.float32,
    )
    left_gb = carried_in((block_decay, fwd_grad), "seq", chain_join, identity, False)[1].astype(
        jnp.bfloat16
    )
    right_gb = carried_in((block_decay, back_grad), "seq", chain_join, identity, True)[1].astype(
        jnp.bfloat16
    )
    query_post = rising * jnp.einsum(
        "the,hde->thd", grad_attn, left_b, preferred_element_type=jnp.float32
    )
    query_post = query_post + shrink * jnp.einsum(
        "the,hde->thd", grad_attn, right_b, preferred_element_type=jnp.float32
    )
    query_post = query_post + jnp.einsum(
        "hts,shd->thd", grad_scores, key_heads, preferred_element_type=jnp.float32
    )
    key_post = rising * jnp.einsum(
        "the,hde->thd", value_heads, left_gb, preferred_element_type=jnp.float32
    )
    key_post = key_post + shrink * jnp.einsum(
        "the,hde->thd", value_heads, right_gb, preferred_element_type=jnp.float32
    )
    key_post = key_post + jnp.einsum(
        "hts,thd->shd", grad_scores, query_heads, preferred_element_type=jnp.float32
    )
    value_post = rising * jnp.einsum(
        "thd,hde->the", key_heads, left_gb, preferred_element_type=jnp.float32
    )
    value_post = value_post + shrink * jnp.einsum(
        "thd,hde->the", key_heads, right_gb, preferred_element_type=jnp.float32
    )
    value_post = value_post + jnp.einsum(
        "hts,the->she", scores, grad_attn, preferred_element_type=jnp.float32
    )
    post_grads = jnp.stack(
        [
            query_post.reshape(tok_rows, channels),
            key_post.reshape(tok_rows, channels),
            value_post.reshape(tok_rows, channels),
        ]
    )
    following = shifted(post_grads[:, :rim_rows].astype(jnp.bfloat16), "seq", -1).astype(
        jnp.float32
    )
    grad_query = filter_back(post_grads[0], following[0], conv_kernel[0]).astype(jnp.bfloat16)
    grad_key = filter_back(post_grads[1], following[1], conv_kernel[1]).astype(jnp.bfloat16)
    grad_value = filter_back(post_grads[2], following[2], conv_kernel[2]).astype(jnp.bfloat16)
    kernel_terms = (
        jnp.stack(
            [
                tap_sums(post_grads[which], raw_rows[which], before[which], kernel_width)
                for which in range(3)
            ]
        )
        * grad_scale
    )
    grad_conv = lax.psum(kernel_terms, ("seq", "rep"))
    partial_x = lax.dot_general(
        grad_value,
        lax.all_gather(value_weight, ("seq", "rep"), axis=0, tiled=True),
        (((1,), (1,)), ((), ())),
        preferred_element_type=jnp.float32,
    )
    grad_x = lax.psum_scatter(
        partial_x[None].astype(jnp.bfloat16), "head", scatter_dimension=2, tiled=True
    )
    columns = gathered
    grad_w = lax.psum_scatter(
        lax.dot_general(
            columns, grad_value, (((0,), (0,)), ((), ())), preferred_element_type=jnp.float32
        )
        * grad_scale,
        ("seq", "rep"),
        scatter_dimension=0,
        tiled=True,
    )
    return (attn_out, grad_query[None], grad_key[None], grad_x, grad_w, grad_conv)


def solution(mesh):
    placed = (
        P(("parts", "rep"), "seq", "head"),
        P(("seq", "rep"), "head"),
        P(("parts", "rep"), "seq", "head"),
        P(("parts", "rep"), "seq", "head"),
        P(("parts", "rep"), "seq", "head"),
        P(None, None, "head"),
        P(("parts", "rep"), "head", "seq"),
    )
    return jax.shard_map(
        local,
        mesh=mesh,
        in_specs=placed,
        out_specs=(
            P(("parts", "rep"), "seq", "head"),
            P(("parts", "rep"), "seq", "head"),
            P(("parts", "rep"), "seq", "head"),
            P(("parts", "rep"), "seq", "head"),
            P(("parts", "seq", "rep"), "head"),
            P("parts", None, "head"),
        ),
        check_vma=False,
    )
```

profile of v0, /device:TPU:0, one launch (start us, length us, event | category | flops | bytes accessed | tf_op | source)
XLA Modules:
  0.0 710.2 jit_solution(15877381056896727067)
XLA Ops:
  11.9 75.4 %all-gather.12.cloned.1.call-done = bf16[2048,2048]{1,0:T(8,128)(2,1)} async-done(((bf16[128,2048]{1,0:T(8,128)(2,1)}), bf16[2048,2048]{1,0:T(8,128)(2,1)}) %all-gather.12.cloned.1.call-update) | async-done | bytes 8388624 | tf_op jit(solution)/shard_map/all_gather | solution.py:108
  87.2 4.6 convolution_convert_fusion.1
  99.2 2.3 fusion.54
  101.6 2.3 copy.108
  105.4 16.3 %all-reduce = f32[128]{0:T(128)S(1)} all-reduce(f32[128]{0:T(128)S(1)} %dynamic-update-slice), channel_id=2, replica_groups=mesh['parts'=2,'seq'=8,'rep'=2,'head'=1] {'seq'}, use_global_device_ids=true, to_apply=%add | all-reduce | flops 128 | bytes 1024
  125.5 2.4 fusion.19
  127.9 54.5 %all-gather.14.cloned.1.call-done = f32[128,128,128]{2,1,0:T(8,128)} async-done(((f32[16,128,128]{2,1,0:T(8,128)}), f32[128,128,128]{2,1,0:T(8,128)}) %all-gather.14.cloned.1.call-update) | async-done | bytes 8388624 | tf_op jit(solution)/shard_map/all_gather | solution.py:21
  183.5 2.6 fusion.18
  186.2 78.5 %all-gather.16.cloned.1.call-done = f32[128,128,128]{2,1,0:T(8,128)} async-done(((f32[16,128,128]{2,1,0:T(8,128)}), f32[128,128,128]{2,1,0:T(8,128)}) %all-gather.16.cloned.1.call-update) | async-done | bytes 8388624 | tf_op jit(solution)/shard_map/all_gather | solution.py:21
  265.8 18.6 %while.57 = (s32[]{:T(128)}, f32[16,128,128]{2,1,0:T(8,128)}, s32[]{:T(128)}, f32[8,16]{1,0:T(8,128)S(1)}, f32[8,16,128,128]{3,2,1,0:T(8,128)}, /*index=5*/s32[]{:T(128)}, s32[]{:T(128)}, s32[]{:T(128)}, s32[]{:T(128)}) while((s32[]{:T(128)}, f32[16,128,128]{2,1,0:T(8,128)}, s32[]{:T(128)}, f32[8,16]{1,0:T(8,128)S(1)}, ...), condition=%wide.region_4.5_spmd, body=%wide.region_3.4_spmd.sunk | while | flops 524294 | bytes 3146075 | solution.py:30
  265.8 2.7 bitcast_add_fusion.5
  268.4 2.7 bitcast_add_fusion.5
  271.1 2.7 bitcast_add_fusion.5
  273.8 2.7 bitcast_add_fusion.5
  276.4 2.7 bitcast_add_fusion.5
  279.1 2.7 bitcast_add_fusion.5
  281.7 2.7 bitcast_add_fusion.5
  291.0 2.3 convolution_convert_fusion.2
  293.9 14.5 %all-reduce.1 = bf16[128]{0:T(256)(128)(2,1)S(1)} all-reduce(bf16[128]{0:T(256)(128)(2,1)S(1)} %dynamic-update-slice.1), channel_id=7, replica_groups=mesh['parts'=2,'seq'=8,'rep'=2,'head'=1] {'seq'}, use_global_device_ids=true, to_apply=%add.1 | all-reduce | flops 128 | bytes 512
  316.6 19.6 %all-gather.18.cloned.1.call-done = bf16[128,128,128]{2,1,0:T(8,128)(2,1)} async-done(((bf16[16,128,128]{2,1,0:T(8,128)(2,1)}), bf16[128,128,128]{2,1,0:T(8,128)(2,1)}) %all-gather.18.cloned.1.call-update) | async-done | bytes 4194320 | tf_op jit(solution)/shard_map/all_gather | solution.py:36
  336.2 20.2 %while.58 = (s32[]{:T(128)}, f32[16,128,128]{2,1,0:T(8,128)}, s32[]{:T(128)}, bf16[8,16]{1,0:T(8,128)(2,1)S(1)}, bf16[8,16,128,128]{3,2,1,0:T(8,128)(2,1)}, /*index=5*/s32[]{:T(128)}, s32[]{:T(128)}) while((s32[]{:T(128)}, f32[16,128,128]{2,1,0:T(8,128)}, s32[]{:T(128)}, bf16[8,16]{1,0:T(8,128)(2,1)S(1)}, ...), condition=%wide.region_8.9_spmd.clone, body=%wide.region_7.8_spmd.clone.sunk | while | flops 1310740 | bytes 2621713 | solution.py:54
  338.5 2.5 fusion.119
  341.0 2.5 fusion.119
  343.6 2.6 fusion.119
  346.2 2.5 fusion.119
  348.8 2.5 fusion.119
  351.3 2.6 fusion.119
  353.9 2.5 fusion.119
  356.4 2.8 fusion.6
  360.7 22.6 %all-gather.20.cloned.1.call-done = bf16[128,128,128]{2,1,0:T(8,128)(2,1)} async-done(((bf16[16,128,128]{2,1,0:T(8,128)(2,1)}), bf16[128,128,128]{2,1,0:T(8,128)(2,1)}) %all-gather.20.cloned.1.call-update) | async-done | bytes 4194320 | tf_op jit(solution)/shard_map/all_gather | solution.py:36
  383.4 20.9 %while.59 = (s32[]{:T(128)}, f32[16,128,128]{2,1,0:T(8,128)}, s32[]{:T(128)}, bf16[8,16]{1,0:T(8,128)(2,1)S(1)}, bf16[8,16,128,128]{3,2,1,0:T(8,128)(2,1)}, /*index=5*/s32[]{:T(128)}, s32[]{:T(128)}, s32[]{:T(128)}, s32[]{:T(128)}) while((s32[]{:T(128)}, f32[16,128,128]{2,1,0:T(8,128)}, s32[]{:T(128)}, ...), condition=%wide.region_10.11_spmd.clone, body=%wide.region_9.10_spmd.clone.sunk | while | flops 1310744 | bytes 2621775 | solution.py:54
  383.4 2.3 fusion.120
  385.7 2.6 fusion.120
  388.3 2.6 fusion.120
  391.0 2.6 fusion.120
  393.6 2.6 fusion.120
  396.3 2.6 fusion.120
  398.9 2.6 fusion.120
  401.6 2.6 fusion.120
  417.7 2.5 copy.157
  420.3 3.6 multiply_reduce_fusion.3
  423.9 8.1 %multiply_bitcast_fusion = f32[2048,2048]{0,1:T(8,128)} fusion(bf16[128,2048]{1,0:T(8,128)(2,1)S(1)} %get-tuple-element.476, bf16[1,128,2048]{2,1,0:T(8,128)(2,1)S(1)} %copy-done), kind=kOutput, calls=%fused_computation.10 | convolution fusion | flops 1077936128 | bytes 17825792 | tf_op jit(solution)/shard_map/dot_general | solution.py:263
  435.7 2.5 copy.126
  438.3 4.3 multiply_reduce_fusion.7
  445.1 8.5 %fusion.2 = bf16[1,128,2048]{2,1,0:T(8,128)(2,1)} fusion(bf16[128,2048]{1,0:T(8,128)(2,1)S(1)} %get-tuple-element.476, bf16[2048,2048]{1,0:T(8,128)(2,1)} %all-gather.12.cloned.1.call-done), kind=kOutput, calls=%fused_computation.13 | convolution fusion | flops 1074003968 | bytes 9437184 | tf_op jit(solution)/shard_map/dot_general | solution.py:252
  453.6 156.4 %reduce-scatter.2.cloned.1.call-done = f32[128,2048]{0,1:T(8,128)} async-done(((f32[2048,2048]{0,1:T(8,128)}), f32[128,2048]{0,1:T(8,128)}) %reduce-scatter.2.cloned.1.call-update) | async-done | bytes 1048592 | tf_op jit(solution)/shard_map/reduce_scatter | solution.py:262
  610.0 2.5 copy.138
  612.5 89.3 %all-reduce.4.cloned.1.call-done = f32[3,4,2048]{2,1,0:T(4,128)} async-done(((f32[3,4,2048]{2,1,0:T(4,128)}), f32[3,4,2048]{2,1,0:T(4,128)}) %all-reduce.4.cloned.1.call-update) | async-done | bytes 98320 | tf_op jit(solution)/shard_map/psum | solution.py:251
  (152 shorter events, 59.2 us)
Async XLA Ops:
  7.2 80.1 %copy-start = (bf16[1,128,2048]{2,1,0:T(8,128)(2,1)S(1)}, bf16[1,128,2048]{2,1,0:T(8,128)(2,1)}, u32[]{:S(2)}) copy-start(bf16[1,128,2048]{2,1,0:T(8,128)(2,1)} %param.15) | copy-start | bytes 1572868
  7.2 80.1 %all-gather.12.cloned.1.call-start = ((), (), s32[]{:S(2)}) async-start(), calls=%async_computation.1 | async-start | bytes 8912896 | tf_op jit(solution)/shard_map/all_gather | solution.py:108
  7.9 174.5 %all-gather.14.cloned.1.call-start = ((), (), s32[]{:S(2)}) async-start(), calls=%async_computation.4 | async-start | bytes 9437184 | tf_op jit(solution)/shard_map/all_gather | solution.py:21
  11.9 83.1 %copy-start.22 = (bf16[1,128,2048]{2,1,0:T(8,128)(2,1)S(1)}, bf16[1,128,2048]{2,1,0:T(8,128)(2,1)}, u32[]{:S(2)}) copy-start(bf16[1,128,2048]{2,1,0:T(8,128)(2,1)} %param.18) | copy-start | bytes 1572868
  92.0 3.0 collective-permute-start
  96.8 1.0 copy-start.12
  97.3 1.9 copy-start.9
  99.2 165.5 %all-gather.16.cloned.1.call-start = ((), (), s32[]{:S(2)}) async-start(), calls=%async_computation.5 | async-start | bytes 9437184 | tf_op jit(solution)/shard_map/all_gather | solution.py:21
  101.5 2.4 copy-start.24
  101.5 20.2 %copy-start.23 = (bf16[1,128,2048]{2,1,0:T(8,128)(2,1)S(1)}, bf16[1,128,2048]{2,1,0:T(8,128)(2,1)}, u32[]{:S(2)}) copy-start(bf16[1,128,2048]{2,1,0:T(8,128)(2,1)} %param.17) | copy-start | bytes 1572868
  101.6 234.7 %all-gather.18.cloned.1.call-start = ((), (), s32[]{:S(2)}) async-start(), calls=%async_computation.6 | async-start | bytes 4718592 | tf_op jit(solution)/shard_map/all_gather | solution.py:36
  121.9 1.1 copy-start.1
  284.4 2.0 copy-start.10
  284.4 2.0 copy-start.20
  286.4 1.2 copy-start.14
  288.8 0.8 copy-start.6
  290.9 92.4 %all-gather.20.cloned.1.call-start = ((), (), s32[]{:S(2)}) async-start(), calls=%async_computation.7 | async-start | bytes 4718592 | tf_op jit(solution)/shard_map/all_gather | solution.py:36
  293.3 316.7 %reduce-scatter.2.cloned.1.call-start = ((), (), s32[]{:S(2)}) async-start(), calls=%async_computation.2 | async-start | bytes 17825792 | tf_op jit(solution)/shard_map/reduce_scatter | solution.py:262
  308.5 1.9 copy-start.4
  308.5 1.9 copy-start.7
  310.4 1.7 copy-start.17
  310.4 1.4 copy-start.3
  311.9 1.0 copy-start.13
  356.4 2.8 copy-start.5
  356.4 2.8 copy-start.11
  404.2 2.1 copy-start.8
  404.2 2.2 copy-start.21
  409.9 2.2 copy-start.18
  413.5 2.1 copy-start.19
  416.4 3.9 collective-permute-start.1
  432.0 2.4 copy-start.15
  432.0 269.8 %all-reduce.4.cloned.1.call-start = ((), (), s32[]{:S(2)}) async-start(), calls=%async_computation.3 | async-start | bytes 196608 | tf_op jit(solution)/shard_map/psum | solution.py:251
  438.3 4.3 copy-start.2
  438.3 4.3 copy-start.16
Sparse Core Ops, SparseCore 0:
  10.2 76.9 all-gather.11
  99.3 83.1 all-gather.13
  184.1 80.5 all-gather.15
  291.1 45.1 all-gather.17
  337.7 45.6 all-gather.19
  432.1 177.8 reduce-scatter.1
  614.0 87.7 all-reduce.3
where the time goes:
time: 712 us; the launch traced here: 710 us
  waiting for transfers between devices  498 us (70%)
  other arithmetic  75.9 us (11%)
  matrix products  51.7 us (7%)
  local copies, waits for them, and re-layouts  34.8 us (5%)
  blocking collectives  30.8 us (4%)
  between operations  15.2 us (2%)
    reduce_scatter x1, waiting for transfers between devices, local(): lax.psum_scatter(lax.dot_general(columns, grad_value, (((0,), (0,)), ((),...  156 us
    all_gather x2, waiting for transfers between devices, prefix(): gathered = jax.tree.map(lambda a: lax.all_gather(a, axis), part)  133 us
    psum x1, waiting for transfers between devices, local(): grad_conv = lax.psum(kernel_terms, ('seq', 'rep'))  89.3 us
    all_gather x1, waiting for transfers between devices, local(): lax.all_gather(value_weight, ('seq', 'rep'), axis=0, tiled=True)  75.4 us
    all_gather x2, waiting for transfers between devices, carried_in(): lax.all_gather(part.astype(kind), axis)  42.3 us
    select_n x16, other arithmetic, step(): return jax.tree.map(lambda a, b: jnp.where(reached, a, b), new, before)  40.9 us
    unnamed x2, blocking collectives  30.8 us
    add x7, other arithmetic, chain_join(): following[0][:, None, None] * earlier[1] + following[1]  18.6 us
  transfers between devices with their start and end apart: 9, of which 8 were waited for; matrix products, arithmetic and copies ran while one was open for 11% of the time, Pallas kernels for 0%

commit v1 on v0

--- a/solution.py
+++ b/solution.py
@@ -52,6 +52,17 @@
         return jax.tree.map(lambda a, b: jnp.where(reached, a, b), new, before)
 
     return lax.fori_loop(0, length, step, start)
+
+
+def scanned(decay, state, axis, reverse):
+    count = lax.axis_size(axis)
+    direction = -1 if reverse else 1
+    distance = 1
+    while distance < count:
+        far_decay, far_state = shifted((decay, state), axis, direction * distance)
+        decay, state = chain_join((far_decay, far_state), (decay, state))
+        distance *= 2
+    return shifted(state, axis, direction)
 
 
 def chain_join(earlier, following):
@@ -155,12 +166,8 @@
         jnp.ones((head_count,), jnp.float32),
         jnp.zeros((head_count, head_size, head_size), jnp.float32),
     )
-    left_b = prefix((block_decay, fwd_sum), "seq", chain_join, identity, False)[1].astype(
-        jnp.bfloat16
-    )
-    right_b = prefix((block_decay, back_sum), "seq", chain_join, identity, True)[1].astype(
-        jnp.bfloat16
-    )
+    left_b = scanned(block_decay, fwd_sum, "seq", False).astype(jnp.bfloat16)
+    right_b = scanned(block_decay, back_sum, "seq", True).astype(jnp.bfloat16)
     attn = rising * jnp.einsum(
         "thd,hde->the", query_heads, left_b, preferred_element_type=jnp.float32
     )
@@ -193,12 +200,8 @@
         grad_attn,
         preferred_element_type=jnp.float32,
     )
-    left_gb = carried_in((block_decay, fwd_grad), "seq", chain_join, identity, False)[1].astype(
-        jnp.bfloat16
-    )
-    right_gb = carried_in((block_decay, back_grad), "seq", chain_join, identity, True)[1].astype(
-        jnp.bfloat16
-    )
+    left_gb = scanned(block_decay, fwd_grad, "seq", False).astype(jnp.bfloat16)
+    right_gb = scanned(block_decay, back_grad, "seq", True).astype(jnp.bfloat16)
     query_post = rising * jnp.einsum(
         "the,hde->thd", grad_attn, left_b, preferred_element_type=jnp.float32
     )
@@ -258,15 +261,16 @@
     grad_x = lax.psum_scatter(
         partial_x[None].astype(jnp.bfloat16), "head", scatter_dimension=2, tiled=True
     )
-    columns = gathered
-    grad_w = lax.psum_scatter(
+    feature_rows = lax.all_to_all(gathered, ("seq", "rep"), 1, 0, tiled=True)
+    grad_value_all = lax.all_gather(grad_value, ("seq", "rep"), axis=0, tiled=True)
+    grad_w = (
         lax.dot_general(
-            columns, grad_value, (((0,), (0,)), ((), ())), preferred_element_type=jnp.float32
-        )
-        * grad_scale,
-        ("seq", "rep"),
-        scatter_dimension=0,
-        tiled=True,
+            feature_rows,
+            grad_value_all,
+            (((0,), (0,)), ((), ())),
+            preferred_element_type=jnp.float32,
+        )
+        * grad_scale
     )
     return (attn_out, grad_query[None], grad_key[None], grad_x, grad_w, grad_conv)
 

time: 712 us -> 548 us (0.77)
  waiting for transfers between devices: 498 us -> 309 us
  starting transfers between devices: 3.96 us -> 98.8 us
  other arithmetic: 75.9 us -> 30.6 us
  matrix products: 51.7 us -> 34.2 us
    reduce_scatter x1 -> x0, waiting for transfers between devices: 156 us -> none  [local(): lax.psum_scatter(lax.dot_general(columns, grad_value, (((0,), (0,)), ((),...]
    all_gather x4 -> x1, waiting for transfers between devices: 175 us -> 33.6 us  [local(): lax.all_gather(grad_value, ('seq', 'rep'), axis=0, tiled=True)]
    ppermute x2 -> x22, waiting for transfers between devices: 0.79 us -> 115 us  [shifted(): return lax.ppermute(block, axis, route)]
    ppermute x2 -> x22, starting transfers between devices: 3.45 us -> 98.7 us  [shifted(): return lax.ppermute(block, axis, route)]
    select_n x16 -> x0, other arithmetic: 40.9 us -> none  [step(): return jax.tree.map(lambda a, b: jnp.where(reached, a, b), new, before)]
    unnamed x2 -> x0, blocking collectives: 30.8 us -> none
    all_to_all x0 -> x1, blocking collectives: none -> 29.8 us  [local(): feature_rows = lax.all_to_all(gathered, ('seq', 'rep'), 1, 0, tiled=True)]
    add x7 -> x10, other arithmetic: 18.6 us -> 12.7 us  [chain_join(): following[0][:, None, None] * earlier[1] + following[1]]
  transfers between devices with their start and end apart: 9 -> 25, of which waited for: 8 -> 16; matrix products, arithmetic and copies ran while one was open for 11% -> 12% of each run, Pallas kernels for 0% -> 0%
where the time goes in v1:
time: 548 us; the launch traced here: 546 us
  waiting for transfers between devices  309 us (56%)
  starting transfers between devices  98.8 us (18%)
  matrix products  34.2 us (6%)
  other arithmetic  30.6 us (6%)
  blocking collectives  29.8 us (5%)
  local copies, waits for them, and re-layouts  29.6 us (5%)
  between operations  14.4 us (3%)
    ppermute x22, waiting for transfers between devices, shifted(): return lax.ppermute(block, axis, route)  115 us
    ppermute x22, starting transfers between devices, shifted(): return lax.ppermute(block, axis, route)  98.7 us
    psum x1, waiting for transfers between devices, local(): grad_conv = lax.psum(kernel_terms, ('seq', 'rep'))  84.3 us
    all_gather x1, waiting for transfers between devices, local(): lax.all_gather(value_weight, ('seq', 'rep'), axis=0, tiled=True)  75.3 us
    all_gather x1, waiting for transfers between devices, local(): lax.all_gather(grad_value, ('seq', 'rep'), axis=0, tiled=True)  33.6 us
    all_to_all x1, blocking collectives, local(): feature_rows = lax.all_to_all(gathered, ('seq', 'rep'), 1, 0, tiled=True)  29.8 us
    add x10, other arithmetic, chain_join(): following[0][:, None, None] * earlier[1] + following[1]  12.7 us
  transfers between devices with their start and end apart: 25, of which 16 were waited for; matrix products, arithmetic and copies ran while one was open for 12% of the time, Pallas kernels for 0%

profile of v1, /device:TPU:0, one launch (start us, length us, event | category | flops | bytes accessed | tf_op | source)
XLA Modules:
  0.0 546.2 jit_solution(14763116871213756074)
XLA Ops:
  11.9 75.3 %all-gather.3.cloned.1.call-done = bf16[2048,2048]{1,0:T(8,128)(2,1)} async-done(((bf16[128,2048]{1,0:T(8,128)(2,1)}), bf16[2048,2048]{1,0:T(8,128)(2,1)}) %all-gather.3.cloned.1.call-update) | async-done | bytes 8388624 | tf_op jit(solution)/shard_map/all_gather | solution.py:119
  87.2 4.6 convolution_convert_fusion.1
  92.0 2.2 collective-permute-start.2
  99.4 3.4 collective-permute-start.3
  105.0 4.4 collective-permute-done.9
  111.2 14.4 %collective-permute-start.4 = (f32[16,128,128]{2,1,0:T(8,128)S(1)}, f32[16,128,128]{2,1,0:T(8,128)S(1)}, u32[]{:S(2)}, u32[]{:S(2)}) collective-permute-start(f32[16,128,128]{2,1,0:T(8,128)S(1)} %get-tuple-element.65), channel_id=1, source_target_pairs={{0,4},{2,6},{4,8},{6,10},{8,12},{10,14},{1,5},{3,7},{5,9},{7,11},{... | collective-permute-start | bytes 3145736 | tf_op jit(solution)/shard_map/ppermute | solution.py:14
  125.6 3.6 collective-permute-start
  130.6 1.7 collective-permute-done.7
  132.3 14.0 %collective-permute-done.10 = f32[16,128,128]{2,1,0:T(8,128)S(1)} collective-permute-done((f32[16,128,128]{2,1,0:T(8,128)S(1)}, f32[16,128,128]{2,1,0:T(8,128)S(1)}, u32[]{:S(2)}, u32[]{:S(2)}) %collective-permute-start.10) | collective-permute-done | bytes 1048608 | tf_op jit(solution)/shard_map/ppermute | solution.py:14
  150.0 10.6 %collective-permute-start.5 = (f32[16,128,128]{2,1,0:T(8,128)}, f32[16,128,128]{2,1,0:T(8,128)}, u32[]{:S(2)}, u32[]{:S(2)}) collective-permute-start(f32[16,128,128]{2,1,0:T(8,128)} %multiply_add_fusion.10), channel_id=1, source_target_pairs={{0,8},{2,10},{4,12},{6,14},{1,9},{3,11},{5,13},{7,15},{16,24},{18,... | collective-permute-start | bytes 3145736 | tf_op jit(solution)/shard_map/ppermute | solution.py:14
  160.6 2.2 copy.108
  162.8 4.0 collective-permute-start.1
  168.1 13.9 %collective-permute-done.1 = f32[16]{0:T(128)S(1)} collective-permute-done((f32[16]{0:T(128)S(1)}, f32[16]{0:T(128)S(1)}, u32[]{:S(2)}, u32[]{:S(2)}) %collective-permute-start.1) | collective-permute-done | bytes 96 | tf_op jit(solution)/shard_map/ppermute | solution.py:14
  183.3 2.0 copy.99
  185.3 1.7 fusion.18
  187.1 14.1 %collective-permute-done.11 = f32[16,128,128]{2,1,0:T(8,128)} collective-permute-done((f32[16,128,128]{2,1,0:T(8,128)}, f32[16,128,128]{2,1,0:T(8,128)}, u32[]{:S(2)}, u32[]{:S(2)}) %collective-permute-start.11) | collective-permute-done | bytes 1048608 | tf_op jit(solution)/shard_map/ppermute | solution.py:14
  201.2 1.7 multiply_add_fusion.6
  204.3 1.7 multiply_add_fusion.9
  206.1 3.2 collective-permute-start.6
  213.6 16.0 %collective-permute-start.13 = (f32[16,128,128]{2,1,0:T(8,128)S(1)}, f32[16,128,128]{2,1,0:T(8,128)S(1)}, u32[]{:S(2)}, u32[]{:S(2)}) collective-permute-start(f32[16,128,128]{2,1,0:T(8,128)S(1)} %fusion.53), channel_id=1, source_target_pairs={{0,2},{2,4},{4,6},{6,8},{8,10},{10,12},{12,14},{1,3},{3,5},{5,7},{... | collective-permute-start | bytes 3145736 | tf_op jit(solution)/shard_map/ppermute | solution.py:14
  231.8 4.3 collective-permute-done.17
  238.0 14.6 %collective-permute-start.14 = (f32[16,128,128]{2,1,0:T(8,128)S(1)}, f32[16,128,128]{2,1,0:T(8,128)S(1)}, u32[]{:S(2)}, u32[]{:S(2)}) collective-permute-start(f32[16,128,128]{2,1,0:T(8,128)S(1)} %get-tuple-element.61), channel_id=1, source_target_pairs={{0,4},{2,6},{4,8},{6,10},{8,12},{10,14},{1,5},{3,7},{5,9},{7,11},{... | collective-permute-start | bytes 3145736 | tf_op jit(solution)/shard_map/ppermute | solution.py:14
  253.4 19.0 %collective-permute-done.18 = f32[16,128,128]{2,1,0:T(8,128)S(1)} collective-permute-done((f32[16,128,128]{2,1,0:T(8,128)S(1)}, f32[16,128,128]{2,1,0:T(8,128)S(1)}, u32[]{:S(2)}, u32[]{:S(2)}) %collective-permute-start.18) | collective-permute-done | bytes 1048608 | tf_op jit(solution)/shard_map/ppermute | solution.py:14
  276.2 9.0 %collective-permute-start.15 = (f32[16,128,128]{2,1,0:T(8,128)}, f32[16,128,128]{2,1,0:T(8,128)}, u32[]{:S(2)}, u32[]{:S(2)}) collective-permute-start(f32[16,128,128]{2,1,0:T(8,128)} %multiply_add_fusion.4), channel_id=1, source_target_pairs={{0,8},{2,10},{4,12},{6,14},{1,9},{3,11},{5,13},{7,15},{16,24},{18,... | collective-permute-start | bytes 3145736 | tf_op jit(solution)/shard_map/ppermute | solution.py:14
  287.2 2.0 copy.156
  290.8 36.1 %collective-permute-done.19 = f32[16,128,128]{2,1,0:T(8,128)} collective-permute-done((f32[16,128,128]{2,1,0:T(8,128)}, f32[16,128,128]{2,1,0:T(8,128)}, u32[]{:S(2)}, u32[]{:S(2)}) %collective-permute-start.19) | collective-permute-done | bytes 1048608 | tf_op jit(solution)/shard_map/ppermute | solution.py:14
  326.9 1.7 multiply_add_fusion
  330.1 1.7 multiply_add_fusion.3
  331.8 3.2 collective-permute-start.16
  336.9 1.7 fusion.90
  338.6 2.0 copy.157
  340.6 1.7 fusion.2
  342.5 1.5 fusion.89
  344.0 2.0 copy.158
  348.1 2.6 copy.159
  350.7 4.3 collective-permute-done.21
  355.0 4.4 multiply_reduce_fusion.3
  359.5 2.0 copy.129
  361.5 29.8 %all_to_all.19 = bf16[128,16,128]{0,2,1:T(8,128)(2,1)} all-to-all(bf16[128,16,128]{0,2,1:T(8,128)(2,1)} %bitcast.200), channel_id=1, replica_groups=mesh['parts'=2,'seq'=8,'rep'=2,'head'=1] {'seq','rep'}, dimensions={1} | all-to-all | bytes 1048576 | tf_op jit(solution)/shard_map/all_to_all | solution.py:264
  391.3 2.0 copy.130
  394.7 2.1 copy.139
  398.2 4.1 multiply_reduce_fusion.11
  402.4 1.7 multiply_reduce_fusion.7
  404.9 8.2 %fusion.1 = bf16[1,128,2048]{2,1,0:T(8,128)(2,1)} fusion(bf16[128,2048]{1,0:T(8,128)(2,1)S(1)} %copy-done.10, bf16[2048,2048]{1,0:T(8,128)(2,1)} %all-gather.3.cloned.1.call-done), kind=kOutput, calls=%fused_computation.4 | convolution fusion | flops 1074003968 | bytes 9437184 | tf_op jit(solution)/shard_map/dot_general | solution.py:255
  413.1 33.6 %all-gather.5.cloned.1.call-done = bf16[2048,2048]{1,0:T(8,128)(2,1)} async-done(((bf16[128,2048]{1,0:T(8,128)(2,1)}), bf16[2048,2048]{1,0:T(8,128)(2,1)}) %all-gather.5.cloned.1.call-update) | async-done | bytes 8388624 | tf_op jit(solution)/shard_map/all_gather | solution.py:265
  446.7 5.8 %fusion = f32[128,2048]{0,1:T(8,128)S(1)} fusion(bf16[2048,2048]{1,0:T(8,128)(2,1)} %all-gather.5.cloned.1.call-done, bf16[2048,128]{1,0:T(8,128)(2,1)S(1)} %bitcast.204), kind=kOutput, calls=%fused_computation.1 | convolution fusion | flops 1074003968 | bytes 9961472 | tf_op jit(solution)/shard_map/dot_general | solution.py:267
  453.8 84.3 %all-reduce.2.cloned.1.call-done = f32[3,4,2048]{2,1,0:T(4,128)} async-done(((f32[3,4,2048]{2,1,0:T(4,128)}), f32[3,4,2048]{2,1,0:T(4,128)}) %all-reduce.2.cloned.1.call-update) | async-done | bytes 98320 | tf_op jit(solution)/shard_map/psum | solution.py:254
  538.1 1.5 copy.188
  (135 shorter events, 49.7 us)
Async XLA Ops:
  7.2 80.1 %copy-start.15 = (bf16[1,128,2048]{2,1,0:T(8,128)(2,1)S(1)}, bf16[1,128,2048]{2,1,0:T(8,128)(2,1)}, u32[]{:S(2)}) copy-start(bf16[1,128,2048]{2,1,0:T(8,128)(2,1)} %param.7) | copy-start | bytes 1572868
  7.2 80.1 %all-gather.3.cloned.1.call-start = ((), (), s32[]{:S(2)}) async-start(), calls=%async_computation.1 | async-start | bytes 8912896 | tf_op jit(solution)/shard_map/all_gather | solution.py:119
  7.9 438.8 %all-gather.5.cloned.1.call-start = ((), (), s32[]{:S(2)}) async-start(), calls=%async_computation.2 | async-start | bytes 8912896 | tf_op jit(solution)/shard_map/all_gather | solution.py:265
  11.9 83.2 %copy-start.23 = (bf16[1,128,2048]{2,1,0:T(8,128)(2,1)S(1)}, bf16[1,128,2048]{2,1,0:T(8,128)(2,1)}, u32[]{:S(2)}) copy-start(bf16[1,128,2048]{2,1,0:T(8,128)(2,1)} %param.10) | copy-start | bytes 1572868
  11.9 83.2 %copy-start.24 = (bf16[1,128,2048]{2,1,0:T(8,128)(2,1)S(1)}, bf16[1,128,2048]{2,1,0:T(8,128)(2,1)}, u32[]{:S(2)}) copy-start(bf16[1,128,2048]{2,1,0:T(8,128)(2,1)} %param.9) | copy-start | bytes 1572868
  91.9 3.1 copy-start.16
  92.0 3.0 collective-permute-start.2
  98.5 4.5 copy-start
  99.4 5.6 %collective-permute-start.3 = (f32[16,128,128]{2,1,0:T(8,128)S(1)}, f32[16,128,128]{2,1,0:T(8,128)S(1)}, u32[]{:S(2)}, u32[]{:S(2)}) collective-permute-start(f32[16,128,128]{2,1,0:T(8,128)S(1)} %fusion.57), channel_id=1, source_target_pairs={{0,2},{2,4},{4,6},{6,8},{8,10},{10,12},{12,14},{1,3},{3,5},{5,7},{... | collective-permute-start | bytes 3145736 | tf_op jit(solution)/shard_map/ppermute | solution.py:14
  103.1 6.3 %collective-permute-start.9 = (f32[16,128,128]{2,1,0:T(8,128)S(1)}, f32[16,128,128]{2,1,0:T(8,128)S(1)}, u32[]{:S(2)}, u32[]{:S(2)}) collective-permute-start(f32[16,128,128]{2,1,0:T(8,128)S(1)} %fusion.55), channel_id=1, source_target_pairs={{2,0},{4,2},{6,4},{8,6},{10,8},{12,10},{14,12},{3,1},{5,3},{7,5},{... | collective-permute-start | bytes 3145736 | tf_op jit(solution)/shard_map/ppermute | solution.py:14
  109.9 36.4 %collective-permute-start.10 = (f32[16,128,128]{2,1,0:T(8,128)S(1)}, f32[16,128,128]{2,1,0:T(8,128)S(1)}, u32[]{:S(2)}, u32[]{:S(2)}) collective-permute-start(f32[16,128,128]{2,1,0:T(8,128)S(1)} %get-tuple-element.66), channel_id=1, source_target_pairs={{4,0},{6,2},{8,4},{10,6},{12,8},{14,10},{5,1},{7,3},{9,5},{11,7},{... | collective-permute-start | bytes 3145736 | tf_op jit(solution)/shard_map/ppermute | solution.py:14
  111.2 37.6 %collective-permute-start.4 = (f32[16,128,128]{2,1,0:T(8,128)S(1)}, f32[16,128,128]{2,1,0:T(8,128)S(1)}, u32[]{:S(2)}, u32[]{:S(2)}) collective-permute-start(f32[16,128,128]{2,1,0:T(8,128)S(1)} %get-tuple-element.65), channel_id=1, source_target_pairs={{0,4},{2,6},{4,8},{6,10},{8,12},{10,14},{1,5},{3,7},{5,9},{7,11},{... | collective-permute-start | bytes 3145736 | tf_op jit(solution)/shard_map/ppermute | solution.py:14
  125.6 4.9 collective-permute-start
  129.3 3.1 collective-permute-start.7
  147.6 53.6 %collective-permute-start.11 = (f32[16,128,128]{2,1,0:T(8,128)}, f32[16,128,128]{2,1,0:T(8,128)}, u32[]{:S(2)}, u32[]{:S(2)}) collective-permute-start(f32[16,128,128]{2,1,0:T(8,128)} %multiply_add_fusion.7), channel_id=1, source_target_pairs={{8,0},{10,2},{12,4},{14,6},{9,1},{11,3},{13,5},{15,7},{24,16},{26,... | collective-permute-start | bytes 3145736 | tf_op jit(solution)/shard_map/ppermute | solution.py:14
  150.0 54.3 %collective-permute-start.5 = (f32[16,128,128]{2,1,0:T(8,128)}, f32[16,128,128]{2,1,0:T(8,128)}, u32[]{:S(2)}, u32[]{:S(2)}) collective-permute-start(f32[16,128,128]{2,1,0:T(8,128)} %multiply_add_fusion.10), channel_id=1, source_target_pairs={{0,8},{2,10},{4,12},{6,14},{1,9},{3,11},{5,13},{7,15},{16,24},{18,... | collective-permute-start | bytes 3145736 | tf_op jit(solution)/shard_map/ppermute | solution.py:14
  162.8 19.2 %collective-permute-start.1 = (f32[16]{0:T(128)S(1)}, f32[16]{0:T(128)S(1)}, u32[]{:S(2)}, u32[]{:S(2)}) collective-permute-start(f32[16]{0:T(128)S(1)} %get-tuple-element.63), channel_id=1, source_target_pairs={{0,4},{2,6},{4,8},{6,10},{8,12},{10,14},{1,5},{3,7},{5,9},{7,11},{... | collective-permute-start | bytes 200 | tf_op jit(solution)/shard_map/ppermute | solution.py:14
  166.8 15.2 %collective-permute-start.8 = (f32[16]{0:T(128)S(1)}, f32[16]{0:T(128)S(1)}, u32[]{:S(2)}, u32[]{:S(2)}) collective-permute-start(f32[16]{0:T(128)S(1)} %get-tuple-element.64), channel_id=1, source_target_pairs={{4,0},{6,2},{8,4},{10,6},{12,8},{14,10},{5,1},{7,3},{9,5},{11,7},{... | collective-permute-start | bytes 200 | tf_op jit(solution)/shard_map/ppermute | solution.py:14
  187.1 22.2 %copy-start.19 = (bf16[16,128,128]{2,1,0:T(8,128)(2,1)}, bf16[16,128,128]{2,1,0:T(8,128)(2,1)S(1)}, u32[]{:S(2)}) copy-start(bf16[16,128,128]{2,1,0:T(8,128)(2,1)S(1)} %fusion.18) | copy-start | bytes 1572868
  202.9 6.4 %copy-start.1 = (bf16[16,16,8,128]{3,2,1,0:T(8,128)(2,1)S(1)}, bf16[16,16,8,128]{3,2,1,0:T(8,128)(2,1)}, u32[]{:S(2)}) copy-start(bf16[16,16,8,128]{3,2,1,0:T(8,128)(2,1)} %copy-done) | copy-start | bytes 1572868
  202.9 6.9 %collective-permute-start.12 = (bf16[16,128,128]{2,1,0:T(8,128)(2,1)S(1)}, bf16[16,128,128]{2,1,0:T(8,128)(2,1)S(1)}, u32[]{:S(2)}, u32[]{:S(2)}) collective-permute-start(bf16[16,128,128]{2,1,0:T(8,128)(2,1)S(1)} %multiply_add_fusion.6), channel_id=1, source_target_pairs={{2,0},{4,2},{6,4},{8,6},{10,8},{12,10},{14,12},{3,1},{5,3},{7,5},{... | collective-permute-start | bytes 1572872 | tf_op jit(solution)/shard_map/ppermute | solution.py:14
  206.1 3.8 copy-start.8
  206.1 4.7 collective-permute-start.6
  212.6 73.1 %copy-start.6 = (bf16[128,16,128]{0,2,1:T(8,128)(2,1)}, bf16[128,16,128]{0,2,1:T(8,128)(2,1)S(1)}, u32[]{:S(2)}) copy-start(bf16[128,16,128]{0,2,1:T(8,128)(2,1)S(1)} %get-tuple-element.36) | copy-start | bytes 1572868
  213.6 18.2 %collective-permute-start.13 = (f32[16,128,128]{2,1,0:T(8,128)S(1)}, f32[16,128,128]{2,1,0:T(8,128)S(1)}, u32[]{:S(2)}, u32[]{:S(2)}) collective-permute-start(f32[16,128,128]{2,1,0:T(8,128)S(1)} %fusion.53), channel_id=1, source_target_pairs={{0,2},{2,4},{4,6},{6,8},{8,10},{10,12},{12,14},{1,3},{3,5},{5,7},{... | collective-permute-start | bytes 3145736 | tf_op jit(solution)/shard_map/ppermute | solution.py:14
  229.6 6.5 %collective-permute-start.17 = (f32[16,128,128]{2,1,0:T(8,128)S(1)}, f32[16,128,128]{2,1,0:T(8,128)S(1)}, u32[]{:S(2)}, u32[]{:S(2)}) collective-permute-start(f32[16,128,128]{2,1,0:T(8,128)S(1)} %fusion.51), channel_id=1, source_target_pairs={{2,0},{4,2},{6,4},{8,6},{10,8},{12,10},{14,12},{3,1},{5,3},{7,5},{... | collective-permute-start | bytes 3145736 | tf_op jit(solution)/shard_map/ppermute | solution.py:14
  236.7 35.7 %collective-permute-start.18 = (f32[16,128,128]{2,1,0:T(8,128)S(1)}, f32[16,128,128]{2,1,0:T(8,128)S(1)}, u32[]{:S(2)}, u32[]{:S(2)}) collective-permute-start(f32[16,128,128]{2,1,0:T(8,128)S(1)} %get-tuple-element.62), channel_id=1, source_target_pairs={{4,0},{6,2},{8,4},{10,6},{12,8},{14,10},{5,1},{7,3},{9,5},{11,7},{... | collective-permute-start | bytes 3145736 | tf_op jit(solution)/shard_map/ppermute | solution.py:14
  238.0 37.1 %collective-permute-start.14 = (f32[16,128,128]{2,1,0:T(8,128)S(1)}, f32[16,128,128]{2,1,0:T(8,128)S(1)}, u32[]{:S(2)}, u32[]{:S(2)}) collective-permute-start(f32[16,128,128]{2,1,0:T(8,128)S(1)} %get-tuple-element.61), channel_id=1, source_target_pairs={{0,4},{2,6},{4,8},{6,10},{8,12},{10,14},{1,5},{3,7},{5,9},{7,11},{... | collective-permute-start | bytes 3145736 | tf_op jit(solution)/shard_map/ppermute | solution.py:14
  253.1 32.1 %copy-start.21 = (bf16[16,128,128]{2,1,0:T(8,128)(2,1)}, bf16[16,128,128]{2,1,0:T(8,128)(2,1)S(1)}, u32[]{:S(2)}) copy-start(bf16[16,128,128]{2,1,0:T(8,128)(2,1)S(1)} %fusion.19) | copy-start | bytes 1572868
  273.6 11.6 %copy-start.4 = (bf16[128,2048]{0,1:T(8,128)(2,1)S(1)}, bf16[128,2048]{0,1:T(8,128)(2,1)}, u32[]{:S(2)}) copy-start(bf16[128,2048]{0,1:T(8,128)(2,1)} %copy.97) | copy-start | bytes 1572868
  273.6 53.3 %collective-permute-start.19 = (f32[16,128,128]{2,1,0:T(8,128)}, f32[16,128,128]{2,1,0:T(8,128)}, u32[]{:S(2)}, u32[]{:S(2)}) collective-permute-start(f32[16,128,128]{2,1,0:T(8,128)} %multiply_add_fusion.1), channel_id=1, source_target_pairs={{8,0},{10,2},{12,4},{14,6},{9,1},{11,3},{13,5},{15,7},{24,16},{26,... | collective-permute-start | bytes 3145736 | tf_op jit(solution)/shard_map/ppermute | solution.py:14
  276.2 53.9 %collective-permute-start.15 = (f32[16,128,128]{2,1,0:T(8,128)}, f32[16,128,128]{2,1,0:T(8,128)}, u32[]{:S(2)}, u32[]{:S(2)}) collective-permute-start(f32[16,128,128]{2,1,0:T(8,128)} %multiply_add_fusion.4), channel_id=1, source_target_pairs={{0,8},{2,10},{4,12},{6,14},{1,9},{3,11},{5,13},{7,15},{16,24},{18,... | collective-permute-start | bytes 3145736 | tf_op jit(solution)/shard_map/ppermute | solution.py:14
  328.6 6.4 %copy-start.7 = (bf16[128,16,128]{0,2,1:T(8,128)(2,1)S(1)}, bf16[128,16,128]{0,2,1:T(8,128)(2,1)}, u32[]{:S(2)}) copy-start(bf16[128,16,128]{0,2,1:T(8,128)(2,1)} %copy-done.6) | copy-start | bytes 1572868
  328.6 6.4 %copy-start.20 = (bf16[16,128,128]{2,1,0:T(8,128)(2,1)S(1)}, bf16[16,128,128]{2,1,0:T(8,128)(2,1)}, u32[]{:S(2)}) copy-start(bf16[16,128,128]{2,1,0:T(8,128)(2,1)} %copy-done.19) | copy-start | bytes 1572868
  328.6 7.8 %collective-permute-start.20 = (bf16[16,128,128]{2,1,0:T(8,128)(2,1)S(1)}, bf16[16,128,128]{2,1,0:T(8,128)(2,1)S(1)}, u32[]{:S(2)}, u32[]{:S(2)}) collective-permute-start(bf16[16,128,128]{2,1,0:T(8,128)(2,1)S(1)} %multiply_add_fusion), channel_id=1, source_target_pairs={{2,0},{4,2},{6,4},{8,6},{10,8},{12,10},{14,12},{3,1},{5,3},{7,5},{... | collective-permute-start | bytes 1572872 | tf_op jit(solution)/shard_map/ppermute | solution.py:14
  331.8 4.6 copy-start.2
  331.8 5.1 collective-permute-start.16
  336.4 2.2 copy-start.22
  340.6 1.7 copy-start.5
  340.6 1.7 copy-start.14
  340.6 1.8 copy-start.18
  346.8 8.2 %collective-permute-start.21 = (bf16[3,3,2048]{2,1,0:T(4,128)(2,1)S(1)}, bf16[3,3,2048]{2,1,0:T(4,128)(2,1)S(1)}, u32[]{:S(2)}, u32[]{:S(2)}) collective-permute-start(bf16[3,3,2048]{2,1,0:T(4,128)(2,1)S(1)} %pad_maximum_fusion.3), channel_id=1, source_target_pairs={{2,0},{4,2},{6,4},{8,6},{10,8},{12,10},{14,12},{3,1},{5,3},{7,5},{... | collective-permute-start | bytes 110600 | tf_op jit(solution)/shard_map/ppermute | solution.py:14
  359.4 178.6 %all-reduce.2.cloned.1.call-start = ((), (), s32[]{:S(2)}) async-start(), calls=%async_computation.3 | async-start | bytes 196608 | tf_op jit(solution)/shard_map/psum | solution.py:254
  361.5 31.9 %copy-start.11 = (f32[128,16,128]{0,2,1:T(8,128)S(1)}, f32[128,16,128]{0,2,1:T(8,128)}, u32[]{:S(2)}) copy-start(f32[128,16,128]{0,2,1:T(8,128)} %get-tuple-element.74) | copy-start | bytes 3145732
  394.7 2.1 copy-start.12
  398.2 4.2 copy-start.13
  402.4 2.5 copy-start.10
  404.9 41.8 %copy-start.25 = (bf16[16,128,128]{2,1,0:T(8,128)(2,1)S(1)}, bf16[16,128,128]{2,1,0:T(8,128)(2,1)}, u32[]{:S(2)}) copy-start(bf16[16,128,128]{2,1,0:T(8,128)(2,1)} %copy.130) | copy-start | bytes 1572868
  (3 other events, 3.9 us)
Sparse Core Ops, SparseCore 0:
  10.2 76.9 all-gather.2
  359.6 87.0 all-gather.4
  450.7 87.3 all-reduce.1

commit v2 on v1

--- a/solution.py
+++ b/solution.py
@@ -63,6 +63,29 @@
         decay, state = chain_join((far_decay, far_state), (decay, state))
         distance *= 2
     return shifted(state, axis, direction)
+
+
+def carried_states(final, sums, axis):
+    count = lax.axis_size(axis)
+    mine = lax.axis_index(axis)
+    finals = lax.all_gather(final, axis)
+    gathered = lax.all_gather(jnp.stack(sums).astype(jnp.bfloat16), axis)
+    blocks = jnp.arange(count)
+    source = blocks[:, None, None]
+    between = blocks[None, :, None]
+    before = (source < between) & (between < mine)
+    after = (mine < between) & (between < source)
+    left_log = jnp.sum(jnp.where(before, finals[None], 0.0), axis=1)
+    right_log = jnp.sum(jnp.where(after, finals[None], 0.0), axis=1)
+    left_weight = jnp.where(blocks[:, None] < mine, jnp.exp(left_log), 0.0)
+    right_weight = jnp.where(blocks[:, None] > mine, jnp.exp(right_log), 0.0)
+    left = jnp.einsum(
+        "ah,ahde->hde", left_weight, gathered[:, 0].astype(jnp.float32)
+    )
+    right = jnp.einsum(
+        "ah,ahde->hde", right_weight, gathered[:, 1].astype(jnp.float32)
+    )
+    return left, right
 
 
 def chain_join(earlier, following):
@@ -166,8 +189,9 @@
         jnp.ones((head_count,), jnp.float32),
         jnp.zeros((head_count, head_size, head_size), jnp.float32),
     )
-    left_b = scanned(block_decay, fwd_sum, "seq", False).astype(jnp.bfloat16)
-    right_b = scanned(block_decay, back_sum, "seq", True).astype(jnp.bfloat16)
+    left_state, right_state = carried_states(final_cum, (fwd_sum, back_sum), "seq")
+    left_b = left_state.astype(jnp.bfloat16)
+    right_b = right_state.astype(jnp.bfloat16)
     attn = rising * jnp.einsum(
         "thd,hde->the", query_heads, left_b, preferred_element_type=jnp.float32
     )
@@ -200,8 +224,9 @@
         grad_attn,
         preferred_element_type=jnp.float32,
     )
-    left_gb = scanned(block_decay, fwd_grad, "seq", False).astype(jnp.bfloat16)
-    right_gb = scanned(block_decay, back_grad, "seq", True).astype(jnp.bfloat16)
+    left_grad, right_grad = carried_states(final_cum, (fwd_grad, back_grad), "seq")
+    left_gb = left_grad.astype(jnp.bfloat16)
+    right_gb = right_grad.astype(jnp.bfloat16)
     query_post = rising * jnp.einsum(
         "the,hde->thd", grad_attn, left_b, preferred_element_type=jnp.float32
     )
@@ -251,7 +276,7 @@
         )
         * grad_scale
     )
-    grad_conv = lax.psum(kernel_terms, ("seq", "rep"))
+    grad_conv = jnp.sum(lax.all_gather(kernel_terms, ("seq", "rep")), axis=0)
     partial_x = lax.dot_general(
         grad_value,
         lax.all_gather(value_weight, ("seq", "rep"), axis=0, tiled=True),

time: 548 us -> 459 us (0.84)
  starting transfers between devices: 98.8 us -> 3.87 us
  waiting for transfers between devices: 309 us -> 290 us
  matrix products: 34.2 us -> 48.8 us
  blocking collectives: 29.8 us -> 38.8 us
  local copies, waits for them, and re-layouts: 29.6 us -> 35.2 us
    all_gather x0 -> x3, waiting for transfers between devices: none -> 140 us  [the longest x2 129 us: carried_states(): gathered = lax.all_gather(jnp.stack(sums).astype(jnp.bfloat16), axis)]
    ppermute x22 -> x2, waiting for transfers between devices: 115 us -> 0.79 us  [shifted(): return lax.ppermute(block, axis, route)]
    ppermute x22 -> x2, starting transfers between devices: 98.7 us -> 3.45 us  [shifted(): return lax.ppermute(block, axis, route)]
    psum x1 -> x0, waiting for transfers between devices: 84.3 us -> none  [local(): grad_conv = lax.psum(kernel_terms, ('seq', 'rep'))]
    all_gather x1, waiting for transfers between devices: 33.6 us -> 73.3 us  [local(): lax.all_gather(grad_value, ('seq', 'rep'), axis=0, tiled=True)]
    unnamed x0 -> x1, blocking collectives: none -> 16.2 us
    add x10 -> x0, other arithmetic: 12.7 us -> none  [chain_join(): following[0][:, None, None] * earlier[1] + following[1]]
    all_to_all x1, blocking collectives: 29.8 us -> 22.6 us  [local(): feature_rows = lax.all_to_all(gathered, ('seq', 'rep'), 1, 0, tiled=True)]
  transfers between devices with their start and end apart: 25 -> 7, of which waited for: 16 -> 6; matrix products, arithmetic and copies ran while one was open for 12% -> 9% of each run, Pallas kernels for 0% -> 0%
where the time goes in v2:
time: 459 us; the launch traced here: 458 us
  waiting for transfers between devices  290 us (63%)
  matrix products  48.8 us (11%)
  blocking collectives  38.8 us (8%)
  local copies, waits for them, and re-layouts  35.2 us (8%)
  other arithmetic  25.9 us (6%)
  between operations  15 us (3%)
    all_gather x2, waiting for transfers between devices, carried_states(): gathered = lax.all_gather(jnp.stack(sums).astype(jnp.bfloat16), axis)  129 us
    all_gather x1, waiting for transfers between devices, local(): lax.all_gather(value_weight, ('seq', 'rep'), axis=0, tiled=True)  75.4 us
    all_gather x1, waiting for transfers between devices, local(): lax.all_gather(grad_value, ('seq', 'rep'), axis=0, tiled=True)  73.3 us
    all_to_all x1, blocking collectives, local(): feature_rows = lax.all_to_all(gathered, ('seq', 'rep'), 1, 0, tiled=True)  22.6 us
    unnamed x1, blocking collectives  16.2 us
    all_gather x1, waiting for transfers between devices, local(): grad_conv = jnp.sum(lax.all_gather(kernel_terms, ('seq', 'rep')), axis=0)  10.4 us
  transfers between devices with their start and end apart: 7, of which 6 were waited for; matrix products, arithmetic and copies ran while one was open for 9% of the time, Pallas kernels for 0%

profile of v2, /device:TPU:0, one launch (start us, length us, event | category | flops | bytes accessed | tf_op | source)
XLA Modules:
  0.0 457.8 jit_solution(11133302419758863520)
XLA Ops:
  10.7 1.2 fusion.98
  11.9 75.4 %all-gather.7.cloned.1.call-done = bf16[2048,2048]{1,0:T(8,128)(2,1)} async-done(((bf16[128,2048]{1,0:T(8,128)(2,1)}), bf16[2048,2048]{1,0:T(8,128)(2,1)}) %all-gather.7.cloned.1.call-update) | async-done | bytes 8388624 | tf_op jit(solution)/shard_map/all_gather | solution.py:142
  87.2 4.8 %convolution_convert_fusion.1 = bf16[128,2048]{1,0:T(8,128)(2,1)S(1)} fusion(bf16[2048,2048]{1,0:T(8,128)(2,1)} %all-gather.7.cloned.1.call-done, bf16[1,128,2048]{2,1,0:T(8,128)(2,1)} %param.7), kind=kOutput, calls=%fused_computation.13 | convolution fusion | flops 1074003968 | bytes 9437184 | tf_op jit(solution)/shard_map/dot_general | solution.py:140
  92.1 2.2 collective-permute-start
  97.0 1.2 maximum_convert_fusion.1
  99.6 1.1 pad_maximum_fusion.3
  102.2 16.2 %all-reduce = f32[128]{0:T(128)S(1)} all-reduce(f32[128]{0:T(128)S(1)} %dynamic-update-slice), channel_id=2, replica_groups=mesh['parts'=2,'seq'=8,'rep'=2,'head'=1] {'seq'}, use_global_device_ids=true, to_apply=%add | all-reduce | flops 128 | bytes 1024
  119.0 2.2 copy.196
  121.2 1.3 add_convert_fusion
  122.4 2.1 copy.188
  124.5 2.5 fusion.22
  127.1 56.9 %all-gather.9.cloned.1.call-done = bf16[8,2,16,128,128]{4,3,2,1,0:T(8,128)(2,1)} async-done(((bf16[1,2,16,128,128]{4,3,2,1,0:T(8,128)(2,1)}), bf16[8,2,16,128,128]{4,3,2,1,0:T(8,128)(2,1)}) %all-gather.9.cloned.1.call-update) | async-done | bytes 8388624 | tf_op jit(solution)/shard_map/all_gather | solution.py:72
  184.0 4.0 slice_bitcast_fusion.2
  188.0 2.8 fusion.2
  191.2 2.8 fusion
  195.7 1.0 divide_convert_fusion
  197.7 1.1 pad_maximum_fusion.4
  199.3 1.9 fusion.23
  201.2 1.8 fusion.17
  203.4 1.6 fusion.101
  205.0 2.1 copy.262
  207.2 72.3 %all-gather.11.cloned.1.call-done = bf16[8,2,16,128,128]{4,3,2,1,0:T(8,128)(2,1)} async-done(((bf16[1,2,16,128,128]{4,3,2,1,0:T(8,128)(2,1)}), bf16[8,2,16,128,128]{4,3,2,1,0:T(8,128)(2,1)}) %all-gather.11.cloned.1.call-update) | async-done | bytes 8388624 | tf_op jit(solution)/shard_map/all_gather | solution.py:72
  279.5 5.6 %multiply_reduce_fusion = (bf16[16,128,128]{2,1,0:T(8,128)(2,1)}, bf16[16,128,128]{2,1,0:T(8,128)(2,1)}) fusion(bf16[8,2,16,128,128]{4,3,2,1,0:T(8,128)(2,1)} %all-gather.11.cloned.1.call-done, f32[16,8]{0,1:T(8,128)S(1)} %fusion.95, f32[16,8]{0,1:T(8,128)S(1)} %fusion.93), kind=kLoop, calls=%fused_computation | loop fusion | flops 12058624 | bytes 9438208
  285.0 2.1 copy.251
  287.1 2.8 fusion.13
  289.9 2.5 fusion.9
  292.4 2.1 copy.258
  294.4 2.1 fusion.12
  296.5 2.6 fusion.100
  299.1 2.1 copy.263
  301.2 1.8 fusion.8
  303.0 2.6 fusion.99
  305.7 2.0 copy.264
  308.5 1.3 collective-permute-start.1
  309.8 2.5 copy.201
  312.4 2.5 copy.214
  314.9 2.6 copy.265
  317.6 4.3 multiply_reduce_fusion.13
  321.9 1.7 multiply_reduce_fusion.9
  323.6 1.7 multiply_reduce_fusion.5
  327.1 22.6 %all_to_all.19 = bf16[128,16,128]{0,2,1:T(8,128)(2,1)S(1)} all-to-all(bf16[128,16,128]{0,2,1:T(8,128)(2,1)S(1)} %bitcast.239), channel_id=1, replica_groups=mesh['parts'=2,'seq'=8,'rep'=2,'head'=1] {'seq','rep'}, dimensions={1} | all-to-all | bytes 1048576 | tf_op jit(solution)/shard_map/all_to_all | solution.py:289
  350.0 1.0 copy.227
  351.0 7.3 %fusion.5 = bf16[1,128,2048]{2,1,0:T(8,128)(2,1)} fusion(bf16[128,2048]{1,0:T(8,128)(2,1)S(1)} %copy-done.11, bf16[2048,2048]{1,0:T(8,128)(2,1)} %all-gather.7.cloned.1.call-done), kind=kOutput, calls=%fused_computation.14 | convolution fusion | flops 1074003968 | bytes 9437184 | tf_op jit(solution)/shard_map/dot_general | solution.py:280
  358.2 10.4 %all-gather.15.cloned.1.call-done = f32[16,3,4,2048]{3,2,1,0:T(4,128)} async-done(((f32[1,3,4,2048]{3,2,1,0:T(4,128)}), f32[16,3,4,2048]{3,2,1,0:T(4,128)}) %all-gather.15.cloned.1.call-update) | async-done | bytes 1572880 | tf_op jit(solution)/shard_map/all_gather | solution.py:279
  368.6 2.4 reduce_sum.177
  370.9 73.3 %all-gather.13.cloned.1.call-done = bf16[2048,2048]{1,0:T(8,128)(2,1)} async-done(((bf16[128,2048]{1,0:T(8,128)(2,1)}), bf16[2048,2048]{1,0:T(8,128)(2,1)}) %all-gather.13.cloned.1.call-update) | async-done | bytes 8388624 | tf_op jit(solution)/shard_map/all_gather | solution.py:290
  444.2 5.8 %fusion.4 = f32[128,2048]{0,1:T(8,128)S(1)} fusion(bf16[2048,2048]{1,0:T(8,128)(2,1)} %all-gather.13.cloned.1.call-done, bf16[2048,128]{1,0:T(8,128)(2,1)S(1)} %bitcast.243), kind=kOutput, calls=%fused_computation.11 | convolution fusion | flops 1074003968 | bytes 9961472 | tf_op jit(solution)/shard_map/dot_general | solution.py:292
  450.0 1.3 copy.228
  (103 shorter events, 15.4 us)
Async XLA Ops:
  7.2 80.1 %all-gather.7.cloned.1.call-start = ((), (), s32[]{:S(2)}) async-start(), calls=%async_computation.1 | async-start | bytes 8912896 | tf_op jit(solution)/shard_map/all_gather | solution.py:142
  7.9 176.1 %all-gather.9.cloned.1.call-start = ((), (), s32[]{:S(2)}) async-start(), calls=%async_computation.2 | async-start | bytes 9437184 | tf_op jit(solution)/shard_map/all_gather | solution.py:72
  11.8 83.3 %copy-start.19 = (bf16[1,128,2048]{2,1,0:T(8,128)(2,1)S(1)}, bf16[1,128,2048]{2,1,0:T(8,128)(2,1)}, u32[]{:S(2)}) copy-start(bf16[1,128,2048]{2,1,0:T(8,128)(2,1)} %param.10) | copy-start | bytes 1572868
  11.9 83.3 %copy-start.20 = (bf16[1,128,2048]{2,1,0:T(8,128)(2,1)S(1)}, bf16[1,128,2048]{2,1,0:T(8,128)(2,1)}, u32[]{:S(2)}) copy-start(bf16[1,128,2048]{2,1,0:T(8,128)(2,1)} %param.9) | copy-start | bytes 1572868
  92.1 3.1 copy-start.15
  92.1 3.0 collective-permute-start
  97.0 1.8 copy-start.3
  98.8 0.8 copy-start.5
  98.8 2.0 copy-start.21
  100.7 178.8 %all-gather.11.cloned.1.call-start = ((), (), s32[]{:S(2)}) async-start(), calls=%async_computation.3 | async-start | bytes 9437184 | tf_op jit(solution)/shard_map/all_gather | solution.py:72
  188.0 2.8 copy-start
  190.8 3.6 copy-start.9
  191.1 3.2 copy-start.6
  191.1 3.2 copy-start.17
  193.9 1.8 copy-start.7
  193.9 1.6 copy-start.10
  196.8 1.0 copy-start.1
  198.9 169.7 %all-gather.15.cloned.1.call-start = ((), (), s32[]{:S(2)}) async-start(), calls=%async_computation.5 | async-start | bytes 1671168 | tf_op jit(solution)/shard_map/all_gather | solution.py:279
  199.1 3.9 copy-start.2
  199.1 3.9 copy-start.8
  199.3 4.1 copy-start.4
  201.2 3.8 copy-start.16
  308.5 9.0 %collective-permute-start.1 = (bf16[3,3,2048]{2,1,0:T(4,128)(2,1)S(1)}, bf16[3,3,2048]{2,1,0:T(4,128)(2,1)S(1)}, u32[]{:S(2)}, u32[]{:S(2)}) collective-permute-start(bf16[3,3,2048]{2,1,0:T(4,128)(2,1)S(1)} %pad_maximum_fusion.5), channel_id=1, source_target_pairs={{2,0},{4,2},{6,4},{8,6},{10,8},{12,10},{14,12},{3,1},{5,3},{7,5},{... | collective-permute-start | bytes 110600 | tf_op jit(solution)/shard_map/ppermute | solution.py:14
  317.5 4.3 copy-start.13
  321.8 1.8 copy-start.12
  323.6 3.2 copy-start.14
  325.3 24.6 %copy-start.18 = (bf16[128,16,128]{0,2,1:T(8,128)(2,1)S(1)}, bf16[128,16,128]{0,2,1:T(8,128)(2,1)}, u32[]{:S(2)}) copy-start(bf16[128,16,128]{0,2,1:T(8,128)(2,1)} %get-tuple-element.55) | copy-start | bytes 1572868
  325.4 25.6 %copy-start.11 = (bf16[128,2048]{1,0:T(8,128)(2,1)S(1)}, bf16[128,2048]{1,0:T(8,128)(2,1)}, u32[]{:S(2)}) copy-start(bf16[128,2048]{1,0:T(8,128)(2,1)} %get-tuple-element.58) | copy-start | bytes 1572868
  326.2 118.1 %all-gather.13.cloned.1.call-start = ((), (), s32[]{:S(2)}) async-start(), calls=%async_computation.4 | async-start | bytes 8912896 | tf_op jit(solution)/shard_map/all_gather | solution.py:290
Sparse Core Ops, SparseCore 0:
  10.2 76.9 all-gather.6
  100.8 83.1 all-gather.8
  199.0 80.4 all-gather.10
  326.3 42.2 all-gather.14
  371.2 72.9 all-gather.12

commit v3 on v2

--- a/solution.py
+++ b/solution.py
@@ -65,10 +65,9 @@
     return shifted(state, axis, direction)
 
 
-def carried_states(final, sums, axis):
+def carried_states(finals, sums, axis):
     count = lax.axis_size(axis)
     mine = lax.axis_index(axis)
-    finals = lax.all_gather(final, axis)
     gathered = lax.all_gather(jnp.stack(sums).astype(jnp.bfloat16), axis)
     blocks = jnp.arange(count)
     source = blocks[:, None, None]
@@ -143,18 +142,13 @@
         preferred_element_type=jnp.float32,
     )
     value_raw = value_f32.astype(jnp.bfloat16)
-    before_all = shifted(
-        jnp.stack(
-            [
-                query_rows[tok_rows - rim_rows :],
-                key_rows[tok_rows - rim_rows :],
-                value_raw[tok_rows - rim_rows :],
-            ]
-        ),
+    before_qk = shifted(
+        jnp.stack([query_rows[tok_rows - rim_rows :], key_rows[tok_rows - rim_rows :]]),
         "seq",
         1,
     )
-    before = (before_all[0], before_all[1], before_all[2])
+    before_value = shifted(value_raw[tok_rows - rim_rows :], "seq", 1)
+    before = (before_qk[0], before_qk[1], before_value)
     raw_rows = (query_rows, key_rows, value_raw)
     convolved = [
         causal_filter(raw_rows[which], before[which], conv_kernel[which]).astype(jnp.bfloat16)
@@ -165,6 +159,11 @@
     value_heads = convolved[2].reshape(tok_rows, head_count, head_size)
     cumulative = jnp.cumsum(log_gate[0], axis=1)
     final_cum = cumulative[:, -1]
+    finals = lax.all_gather(final_cum, "seq")
+    feature_rows = lax.all_to_all(gathered, ("seq", "rep"), 1, 0, tiled=True)
+    finals, feature_rows, query_heads, key_heads = lax.optimization_barrier(
+        (finals, feature_rows, query_heads, key_heads)
+    )
     block_decay = jnp.exp(final_cum)
     rising = jnp.exp(cumulative).T[:, :, None]
     shrink = jnp.exp(final_cum[:, None] - cumulative).T[:, :, None]
@@ -189,7 +188,7 @@
         jnp.ones((head_count,), jnp.float32),
         jnp.zeros((head_count, head_size, head_size), jnp.float32),
     )
-    left_state, right_state = carried_states(final_cum, (fwd_sum, back_sum), "seq")
+    left_state, right_state = carried_states(finals, (fwd_sum, back_sum), "seq")
     left_b = left_state.astype(jnp.bfloat16)
     right_b = right_state.astype(jnp.bfloat16)
     attn = rising * jnp.einsum(
@@ -224,7 +223,7 @@
         grad_attn,
         preferred_element_type=jnp.float32,
     )
-    left_grad, right_grad = carried_states(final_cum, (fwd_grad, back_grad), "seq")
+    left_grad, right_grad = carried_states(finals, (fwd_grad, back_grad), "seq")
     left_gb = left_grad.astype(jnp.bfloat16)
     right_gb = right_grad.astype(jnp.bfloat16)
     query_post = rising * jnp.einsum(
@@ -286,7 +285,6 @@
     grad_x = lax.psum_scatter(
         partial_x[None].astype(jnp.bfloat16), "head", scatter_dimension=2, tiled=True
     )
-    feature_rows = lax.all_to_all(gathered, ("seq", "rep"), 1, 0, tiled=True)
     grad_value_all = lax.all_gather(grad_value, ("seq", "rep"), axis=0, tiled=True)
     grad_w = (
         lax.dot_general(

time: 459 us -> 467 us (1.017)
  blocking collectives: 38.8 us -> 25.2 us
  starting transfers between devices: 3.87 us -> 13.9 us
  waiting for transfers between devices: 290 us -> 299 us
    all_gather x1, waiting for transfers between devices: 75.4 us -> 45.5 us  [local(): lax.all_gather(value_weight, ('seq', 'rep'), axis=0, tiled=True)]
    all_to_all x1 -> x0, blocking collectives: 22.6 us -> none  [local(): feature_rows = lax.all_to_all(gathered, ('seq', 'rep'), 1, 0, tiled=True)]
    all_gather x1, waiting for transfers between devices: 10.4 us -> 31.3 us  [local(): grad_conv = jnp.sum(lax.all_gather(kernel_terms, ('seq', 'rep')), axis=0)]
    all_gather x2, waiting for transfers between devices: 129 us -> 148 us  [carried_states(): gathered = lax.all_gather(jnp.stack(sums).astype(jnp.bfloat16), axis)]
    unnamed x1, blocking collectives: 16.2 us -> 25.2 us
    all_to_all x0 -> x1, starting transfers between devices: none -> 7.23 us  [local(): feature_rows = lax.all_to_all(gathered, ('seq', 'rep'), 1, 0, tiled=True)]
  transfers between devices with their start and end apart: 7 -> 9, of which waited for: 6 -> 5; matrix products, arithmetic and copies ran while one was open for 9% -> 11% of each run, Pallas kernels for 0% -> 0%
where the time goes in v3:
time: 467 us; the launch traced here: 466 us
  waiting for transfers between devices  299 us (64%)
  matrix products  48.5 us (10%)
  local copies, waits for them, and re-layouts  37.7 us (8%)
  other arithmetic  26.4 us (6%)
  blocking collectives  25.2 us (5%)
  between operations  14.9 us (3%)
  starting transfers between devices  13.9 us (3%)
    all_gather x2, waiting for transfers between devices, carried_states(): gathered = lax.all_gather(jnp.stack(sums).astype(jnp.bfloat16), axis)  148 us
    all_gather x1, waiting for transfers between devices, local(): lax.all_gather(grad_value, ('seq', 'rep'), axis=0, tiled=True)  73.3 us
    all_gather x1, waiting for transfers between devices, local(): lax.all_gather(value_weight, ('seq', 'rep'), axis=0, tiled=True)  45.5 us
    all_gather x1, waiting for transfers between devices, local(): grad_conv = jnp.sum(lax.all_gather(kernel_terms, ('seq', 'rep')), axis=0)  31.3 us
    unnamed x1, blocking collectives  25.2 us
  transfers between devices with their start and end apart: 9, of which 5 were waited for; matrix products, arithmetic and copies ran while one was open for 11% of the time, Pallas kernels for 0%

profile of v3, /device:TPU:0, one launch (start us, length us, event | category | flops | bytes accessed | tf_op | source)
XLA Modules:
  0.0 465.6 jit_solution(15122210084729881408)
XLA Ops:
  9.5 2.4 collective-permute-start
  11.9 2.0 copy.181
  13.9 7.2 %all-to-all-start = ((bf16[128,16,128]{0,2,1:T(8,128)(2,1)}), bf16[128,16,128]{0,2,1:T(8,128)(2,1)}, u32[]{:S(2)}, u32[]{:S(2)}) async-start(bf16[128,16,128]{0,2,1:T(8,128)(2,1)} %bitcast.7), calls=%async_computation | async-start | bytes 1048576 | tf_op jit(solution)/shard_map/all_to_all | solution.py:163
  22.4 1.1 fusion.97
  23.6 1.2 dynamic-slice
  25.7 25.2 %all-reduce = f32[128]{0:T(128)S(1)} all-reduce(f32[128]{0:T(128)S(1)} %dynamic-update-slice), channel_id=2, replica_groups=mesh['parts'=2,'seq'=8,'rep'=2,'head'=1] {'seq'}, use_global_device_ids=true, to_apply=%add | all-reduce | flops 128 | bytes 1024
  51.1 1.5 maximum_convert_fusion
  53.1 45.5 %all-gather.7.cloned.1.call-done = bf16[2048,2048]{1,0:T(8,128)(2,1)} async-done(((bf16[128,2048]{1,0:T(8,128)(2,1)}), bf16[2048,2048]{1,0:T(8,128)(2,1)}) %all-gather.7.cloned.1.call-update) | async-done | bytes 8388624 | tf_op jit(solution)/shard_map/all_gather | solution.py:141
  98.6 4.6 convolution_convert_fusion.1
  104.1 2.2 collective-permute-start.1
  108.7 2.0 copy.182
  110.7 1.2 maximum_convert_fusion.2
  113.3 1.1 pad_maximum_fusion.3
  114.6 2.2 copy.194
  117.3 2.5 fusion.21
  119.9 75.4 %all-gather.9.cloned.1.call-done = bf16[8,2,16,128,128]{4,3,2,1,0:T(8,128)(2,1)} async-done(((bf16[1,2,16,128,128]{4,3,2,1,0:T(8,128)(2,1)}), bf16[8,2,16,128,128]{4,3,2,1,0:T(8,128)(2,1)}) %all-gather.9.cloned.1.call-update) | async-done | bytes 8388624 | tf_op jit(solution)/shard_map/all_gather | solution.py:71
  195.2 4.0 slice_bitcast_fusion.2
  199.3 2.8 fusion.2
  202.4 2.8 fusion
  209.1 1.1 pad_maximum_fusion.4
  210.6 1.9 fusion.22
  212.5 1.8 fusion.16
  214.7 1.6 fusion.100
  216.4 2.1 copy.257
  218.5 72.4 %all-gather.11.cloned.1.call-done = bf16[8,2,16,128,128]{4,3,2,1,0:T(8,128)(2,1)} async-done(((bf16[1,2,16,128,128]{4,3,2,1,0:T(8,128)(2,1)}), bf16[8,2,16,128,128]{4,3,2,1,0:T(8,128)(2,1)}) %all-gather.11.cloned.1.call-update) | async-done | bytes 8388624 | tf_op jit(solution)/shard_map/all_gather | solution.py:71
  290.8 5.6 %multiply_reduce_fusion = (bf16[16,128,128]{2,1,0:T(8,128)(2,1)}, bf16[16,128,128]{2,1,0:T(8,128)(2,1)}) fusion(bf16[8,2,16,128,128]{4,3,2,1,0:T(8,128)(2,1)} %all-gather.11.cloned.1.call-done, f32[16,8]{0,1:T(8,128)S(1)} %fusion.94, f32[16,8]{0,1:T(8,128)S(1)} %fusion.92), kind=kLoop, calls=%fused_computation | loop fusion | flops 12058624 | bytes 9438208
  296.4 2.1 copy.246
  298.5 2.8 fusion.12
  301.3 2.5 fusion.8
  303.7 2.1 copy.253
  305.8 2.1 fusion.11
  307.9 2.6 fusion.99
  310.5 2.1 copy.258
  312.6 1.8 fusion.7
  314.4 2.6 fusion.98
  317.0 2.0 copy.259
  319.9 1.3 collective-permute-start.2
  321.2 2.5 copy.199
  323.7 2.5 copy.212
  326.3 2.6 copy.260
  328.9 4.3 multiply_reduce_fusion.13
  333.2 1.7 multiply_reduce_fusion.9
  335.0 1.7 multiply_reduce_fusion.5
  339.2 7.3 %fusion.4 = bf16[1,128,2048]{2,1,0:T(8,128)(2,1)} fusion(bf16[128,2048]{1,0:T(8,128)(2,1)} %get-tuple-element.66, bf16[2048,2048]{1,0:T(8,128)(2,1)} %all-gather.7.cloned.1.call-done), kind=kOutput, calls=%fused_computation.13 | convolution fusion | flops 1074003968 | bytes 9437184 | tf_op jit(solution)/shard_map/dot_general | solution.py:279
  346.5 31.3 %all-gather.15.cloned.1.call-done = f32[16,3,4,2048]{3,2,1,0:T(4,128)} async-done(((f32[1,3,4,2048]{3,2,1,0:T(4,128)}), f32[16,3,4,2048]{3,2,1,0:T(4,128)}) %all-gather.15.cloned.1.call-update) | async-done | bytes 1572880 | tf_op jit(solution)/shard_map/all_gather | solution.py:278
  377.8 2.4 reduce_sum.177
  380.1 73.3 %all-gather.13.cloned.1.call-done = bf16[2048,2048]{1,0:T(8,128)(2,1)} async-done(((bf16[128,2048]{1,0:T(8,128)(2,1)}), bf16[2048,2048]{1,0:T(8,128)(2,1)}) %all-gather.13.cloned.1.call-update) | async-done | bytes 8388624 | tf_op jit(solution)/shard_map/all_gather | solution.py:288
  453.4 5.6 %convolution_multiply_fusion = f32[128,2048]{1,0:T(8,128)} fusion(bf16[2048,128]{1,0:T(8,128)(2,1)S(1)} %bitcast.229, bf16[2048,2048]{1,0:T(8,128)(2,1)} %all-gather.13.cloned.1.call-done), kind=kOutput, calls=%fused_computation.10 | convolution fusion | flops 1074003968 | bytes 9961472 | tf_op jit(solution)/shard_map/dot_general | solution.py:290
  (99 shorter events, 17.7 us)
Async XLA Ops:
  7.2 91.4 %all-gather.7.cloned.1.call-start = ((), (), s32[]{:S(2)}) async-start(), calls=%async_computation.1 | async-start | bytes 8912896 | tf_op jit(solution)/shard_map/all_gather | solution.py:141
  9.5 41.6 %collective-permute-start = (bf16[2,3,2048]{2,1,0:T(4,128)(2,1)S(1)}, bf16[2,3,2048]{2,1,0:T(4,128)(2,1)S(1)}, u32[]{:S(2)}, u32[]{:S(2)}) collective-permute-start(bf16[2,3,2048]{2,1,0:T(4,128)(2,1)S(1)} %pad_maximum_fusion.7), channel_id=1, source_target_pairs={{0,2},{2,4},{4,6},{6,8},{8,10},{10,12},{12,14},{1,3},{3,5},{5,7},{... | collective-permute-start | bytes 73736 | tf_op jit(solution)/shard_map/ppermute | solution.py:14
  13.9 94.8 %all-to-all-start = ((bf16[128,16,128]{0,2,1:T(8,128)(2,1)}), bf16[128,16,128]{0,2,1:T(8,128)(2,1)}, u32[]{:S(2)}, u32[]{:S(2)}) async-start(bf16[128,16,128]{0,2,1:T(8,128)(2,1)} %bitcast.7), calls=%async_computation | async-start | bytes 1048576 | tf_op jit(solution)/shard_map/all_to_all | solution.py:163
  21.2 174.1 %all-gather.9.cloned.1.call-start = ((), (), s32[]{:S(2)}) async-start(), calls=%async_computation.2 | async-start | bytes 9437184 | tf_op jit(solution)/shard_map/all_gather | solution.py:71
  22.4 76.2 %copy-start.13 = (bf16[1,128,2048]{2,1,0:T(8,128)(2,1)S(1)}, bf16[1,128,2048]{2,1,0:T(8,128)(2,1)}, u32[]{:S(2)}) copy-start(bf16[1,128,2048]{2,1,0:T(8,128)(2,1)} %param.7) | copy-start | bytes 1572868
  103.3 0.8 copy-start.15
  104.1 6.7 %collective-permute-start.1 = (bf16[3,2048]{1,0:T(4,128)(2,1)S(1)}, bf16[3,2048]{1,0:T(4,128)(2,1)S(1)}, u32[]{:S(2)}, u32[]{:S(2)}) collective-permute-start(bf16[3,2048]{1,0:T(4,128)(2,1)S(1)} %slice.256), channel_id=1, source_target_pairs={{0,2},{2,4},{4,6},{6,8},{8,10},{10,12},{12,14},{1,3},{3,5},{5,7},{... | collective-permute-start | bytes 36872 | tf_op jit(solution)/shard_map/ppermute | solution.py:14
  110.7 1.8 copy-start.3
  112.5 0.8 copy-start.5
  114.4 176.4 %all-gather.11.cloned.1.call-start = ((), (), s32[]{:S(2)}) async-start(), calls=%async_computation.3 | async-start | bytes 9437184 | tf_op jit(solution)/shard_map/all_gather | solution.py:71
  199.3 2.8 copy-start
  202.0 3.6 copy-start.10
  202.4 3.2 copy-start.6
  202.4 3.2 copy-start.17
  205.2 1.8 copy-start.7
  205.2 1.6 copy-start.9
  208.1 1.0 copy-start.1
  210.2 167.6 %all-gather.15.cloned.1.call-start = ((), (), s32[]{:S(2)}) async-start(), calls=%async_computation.5 | async-start | bytes 1671168 | tf_op jit(solution)/shard_map/all_gather | solution.py:278
  210.4 3.9 copy-start.2
  210.4 3.9 copy-start.8
  210.6 4.1 copy-start.4
  212.5 3.8 copy-start.16
  319.9 9.0 %collective-permute-start.2 = (bf16[3,3,2048]{2,1,0:T(4,128)(2,1)S(1)}, bf16[3,3,2048]{2,1,0:T(4,128)(2,1)S(1)}, u32[]{:S(2)}, u32[]{:S(2)}) collective-permute-start(bf16[3,3,2048]{2,1,0:T(4,128)(2,1)S(1)} %pad_maximum_fusion.5), channel_id=1, source_target_pairs={{2,0},{4,2},{6,4},{8,6},{10,8},{12,10},{14,12},{3,1},{5,3},{7,5},{... | collective-permute-start | bytes 110600 | tf_op jit(solution)/shard_map/ppermute | solution.py:14
  328.9 4.3 copy-start.12
  333.2 1.8 copy-start.11
  335.0 3.2 copy-start.18
  337.6 115.9 %all-gather.13.cloned.1.call-start = ((), (), s32[]{:S(2)}) async-start(), calls=%async_computation.4 | async-start | bytes 8912896 | tf_op jit(solution)/shard_map/all_gather | solution.py:288
  339.2 114.3 %copy-start.14 = (bf16[16,128,128]{2,1,0:T(8,128)(2,1)S(1)}, bf16[16,128,128]{2,1,0:T(8,128)(2,1)}, u32[]{:S(2)}) copy-start(bf16[16,128,128]{2,1,0:T(8,128)(2,1)} %copy.182) | copy-start | bytes 1572868
Sparse Core Ops, SparseCore 0:
  10.2 88.3 all-gather.6
  114.5 80.6 all-gather.8
  210.3 80.5 all-gather.10
  337.7 40.0 all-gather.14
  380.4 72.9 all-gather.12

commit v4 on v2

--- a/solution.py
+++ b/solution.py
@@ -65,11 +65,30 @@
     return shifted(state, axis, direction)
 
 
-def carried_states(final, sums, axis):
+def split_exact(x):
+    high = x.astype(jnp.bfloat16)
+    rest = x - high.astype(jnp.float32)
+    middle = rest.astype(jnp.bfloat16)
+    low = (rest - middle.astype(jnp.float32)).astype(jnp.bfloat16)
+    return jnp.stack([high, middle, low])
+
+
+def carried_states(final, sums, axis, finals=None):
     count = lax.axis_size(axis)
     mine = lax.axis_index(axis)
-    finals = lax.all_gather(final, axis)
-    gathered = lax.all_gather(jnp.stack(sums).astype(jnp.bfloat16), axis)
+    stacked = jnp.stack(sums).astype(jnp.bfloat16)
+    width = stacked.shape[-1]
+    rows = stacked.size // width
+    heads = final.shape[0]
+    if finals is None:
+        extra = jnp.zeros((16, width), jnp.bfloat16).at[:3, :heads].set(split_exact(final))
+        payload = jnp.concatenate([stacked.reshape(rows, width), extra])
+        packed = lax.all_gather(payload, axis)
+        pieces = packed[:, rows : rows + 3, :heads].astype(jnp.float32)
+        finals = (pieces[:, 0] + pieces[:, 1]) + pieces[:, 2]
+        gathered = packed[:, :rows].reshape((count,) + stacked.shape)
+    else:
+        gathered = lax.all_gather(stacked, axis)
     blocks = jnp.arange(count)
     source = blocks[:, None, None]
     between = blocks[None, :, None]
@@ -85,7 +104,7 @@
     right = jnp.einsum(
         "ah,ahde->hde", right_weight, gathered[:, 1].astype(jnp.float32)
     )
-    return left, right
+    return left, right, finals
 
 
 def chain_join(earlier, following):
@@ -189,7 +208,7 @@
         jnp.ones((head_count,), jnp.float32),
         jnp.zeros((head_count, head_size, head_size), jnp.float32),
     )
-    left_state, right_state = carried_states(final_cum, (fwd_sum, back_sum), "seq")
+    left_state, right_state, finals = carried_states(final_cum, (fwd_sum, back_sum), "seq")
     left_b = left_state.astype(jnp.bfloat16)
     right_b = right_state.astype(jnp.bfloat16)
     attn = rising * jnp.einsum(
@@ -224,7 +243,7 @@
         grad_attn,
         preferred_element_type=jnp.float32,
     )
-    left_grad, right_grad = carried_states(final_cum, (fwd_grad, back_grad), "seq")
+    left_grad, right_grad, _ = carried_states(final_cum, (fwd_grad, back_grad), "seq", finals)
     left_gb = left_grad.astype(jnp.bfloat16)
     right_gb = right_grad.astype(jnp.bfloat16)
     query_post = rising * jnp.einsum(

time: 459 us -> 473 us (1.031)
  waiting for transfers between devices: 290 us -> 309 us
  blocking collectives: 38.8 us -> 22.6 us
  local copies, waits for them, and re-layouts: 35.2 us -> 42.7 us
    all_gather x2, waiting for transfers between devices: 129 us -> 147 us  [the longest x1 75.1 us: carried_states(): packed = lax.all_gather(payload, axis)]
    unnamed x1 -> x0, blocking collectives: 16.2 us -> none
    slice x0 -> x1, local copies, waits for them, and re-layouts: none -> 7.2 us  [carried_states(): gathered = packed[:, :rows].reshape((count,) + stacked.shape)]
  transfers between devices with their start and end apart: 7 -> 7, of which waited for: 6 -> 6; matrix products, arithmetic and copies ran while one was open for 9% -> 8% of each run, Pallas kernels for 0% -> 0%
where the time goes in v4:
time: 473 us; the launch traced here: 471 us
  waiting for transfers between devices  309 us (65%)
  matrix products  52.1 us (11%)
  local copies, waits for them, and re-layouts  42.7 us (9%)
  other arithmetic  27 us (6%)
  blocking collectives  22.6 us (5%)
  between operations  14.3 us (3%)
    all_gather x1, waiting for transfers between devices, local(): lax.all_gather(value_weight, ('seq', 'rep'), axis=0, tiled=True)  75.3 us
    all_gather x1, waiting for transfers between devices, carried_states(): packed = lax.all_gather(payload, axis)  75.1 us
    all_gather x1, waiting for transfers between devices, local(): lax.all_gather(grad_value, ('seq', 'rep'), axis=0, tiled=True)  73.3 us
    all_gather x1, waiting for transfers between devices, carried_states(): gathered = lax.all_gather(stacked, axis)  72.4 us
    all_to_all x1, blocking collectives, local(): feature_rows = lax.all_to_all(gathered, ('seq', 'rep'), 1, 0, tiled=True)  22.6 us
    all_gather x1, waiting for transfers between devices, local(): grad_conv = jnp.sum(lax.all_gather(kernel_terms, ('seq', 'rep')), axis=0)  10.3 us
  transfers between devices with their start and end apart: 7, of which 6 were waited for; matrix products, arithmetic and copies ran while one was open for 8% of the time, Pallas kernels for 0%

profile of v4, /device:TPU:0, one launch (start us, length us, event | category | flops | bytes accessed | tf_op | source)
XLA Modules:
  0.0 471.2 jit_solution(18010945671634118290)
XLA Ops:
  10.8 1.2 fusion.108
  12.0 75.3 %all-gather.7.cloned.1.call-done = bf16[2048,2048]{1,0:T(8,128)(2,1)} async-done(((bf16[128,2048]{1,0:T(8,128)(2,1)}), bf16[2048,2048]{1,0:T(8,128)(2,1)}) %all-gather.7.cloned.1.call-update) | async-done | bytes 8388624 | tf_op jit(solution)/shard_map/all_gather | solution.py:161
  87.2 4.8 %convolution_convert_fusion.1 = bf16[128,2048]{1,0:T(8,128)(2,1)S(1)} fusion(bf16[2048,2048]{1,0:T(8,128)(2,1)} %all-gather.7.cloned.1.call-done, bf16[1,128,2048]{2,1,0:T(8,128)(2,1)} %param.9), kind=kOutput, calls=%fused_computation.13 | convolution fusion | flops 1074003968 | bytes 9437184 | tf_op jit(solution)/shard_map/dot_general | solution.py:159
  92.1 2.2 collective-permute-start
  97.0 1.2 maximum_convert_fusion.1
  99.7 1.1 pad_maximum_fusion
  101.0 2.2 copy.196
  103.2 1.3 add_convert_fusion
  104.5 2.0 copy.188
  106.5 2.5 fusion.22
  109.1 75.1 %all-gather.15.cloned.1.call-done = bf16[32896,128]{1,0:T(8,128)(2,1)} async-done(((bf16[4112,128]{1,0:T(8,128)(2,1)}), bf16[32896,128]{1,0:T(8,128)(2,1)}) %all-gather.15.cloned.1.call-update) | async-done | bytes 8421392 | tf_op jit(solution)/shard_map/all_gather | solution.py:86
  184.9 7.2 %slice.305 = bf16[8,4096,128]{2,1,0:T(8,128)(2,1)} slice(bf16[8,4112,128]{2,1,0:T(8,128)(2,1)} %bitcast.250), slice={[0:8], [0:4096], [0:128]} | slice | bytes 16777216 | tf_op jit(solution)/shard_map/slice | solution.py:89
  192.4 5.3 %slice_bitcast_fusion.2 = (bf16[8,16,128,128]{3,2,1,0:T(8,128)(2,1)}, bf16[8,16,128,128]{3,2,1,0:T(8,128)(2,1)S(1)}) fusion(bf16[8,2,16,128,128]{4,3,2,1,0:T(8,128)(2,1)} %bitcast.230), kind=kLoop, calls=%fused_computation.4 | loop fusion | bytes 16777216 | tf_op jit(solution)/shard_map/squeeze | solution.py:105
  197.7 2.8 fusion.2
  200.5 1.3 fusion.21
  202.0 5.1 %fusion = f32[16,1,128,128]{3,1,2,0:T(1,128)S(1)} fusion(bf16[8,16,1,1]{0,2,3,1:T(2,128)(2,1)S(1)} %copy.234, bf16[8,16,128,128]{3,2,1,0:T(8,128)(2,1)} %get-tuple-element.64), kind=kOutput, calls=%fused_computation.6 | convolution fusion | flops 4194304 | bytes 5243136 | tf_op jit(solution)/shard_map/ah,ahde->hde/dot_general | solution.py:104
  208.9 1.0 divide_convert_fusion
  210.9 1.1 pad_maximum_fusion.5
  212.3 1.9 fusion.23
  214.3 1.8 fusion.17
  216.4 1.6 fusion.111
  218.1 2.1 copy.262
  220.3 72.4 %all-gather.9.cloned.1.call-done = bf16[8,2,16,128,128]{4,3,2,1,0:T(8,128)(2,1)} async-done(((bf16[1,2,16,128,128]{4,3,2,1,0:T(8,128)(2,1)}), bf16[8,2,16,128,128]{4,3,2,1,0:T(8,128)(2,1)}) %all-gather.9.cloned.1.call-update) | async-done | bytes 8388624 | tf_op jit(solution)/shard_map/all_gather | solution.py:91
  292.7 5.5 %multiply_reduce_fusion = (bf16[16,128,128]{2,1,0:T(8,128)(2,1)}, bf16[16,128,128]{2,1,0:T(8,128)(2,1)}) fusion(bf16[8,2,16,128,128]{4,3,2,1,0:T(8,128)(2,1)} %all-gather.9.cloned.1.call-done, f32[16,8]{0,1:T(8,128)S(1)} %fusion.104, f32[16,8]{0,1:T(8,128)S(1)} %fusion.102), kind=kLoop, calls=%fused_computation | loop fusion | flops 12058624 | bytes 9438208
  298.2 2.1 copy.251
  300.3 2.5 fusion.9
  302.8 2.8 fusion.13
  305.5 2.1 copy.258
  307.6 1.8 fusion.8
  309.4 2.6 fusion.109
  312.1 2.0 copy.264
  314.1 2.1 fusion.12
  316.2 2.6 fusion.110
  318.8 2.0 copy.263
  321.7 1.3 collective-permute-start.1
  323.0 2.6 copy.201
  325.6 2.5 copy.214
  328.1 2.5 copy.265
  330.7 4.5 multiply_reduce_fusion.13
  335.2 1.7 multiply_reduce_fusion.9
  337.0 1.7 multiply_reduce_fusion.5
  340.4 22.6 %all_to_all.19 = bf16[128,16,128]{0,2,1:T(8,128)(2,1)S(1)} all-to-all(bf16[128,16,128]{0,2,1:T(8,128)(2,1)S(1)} %bitcast.259), channel_id=1, replica_groups=mesh['parts'=2,'seq'=8,'rep'=2,'head'=1] {'seq','rep'}, dimensions={1} | all-to-all | bytes 1048576 | tf_op jit(solution)/shard_map/all_to_all | solution.py:308
  364.4 7.3 %fusion.5 = bf16[1,128,2048]{2,1,0:T(8,128)(2,1)} fusion(bf16[128,2048]{1,0:T(8,128)(2,1)S(1)} %copy-done.12, bf16[2048,2048]{1,0:T(8,128)(2,1)} %all-gather.7.cloned.1.call-done), kind=kOutput, calls=%fused_computation.14 | convolution fusion | flops 1074003968 | bytes 9437184 | tf_op jit(solution)/shard_map/dot_general | solution.py:299
  371.6 10.3 %all-gather.13.cloned.1.call-done = f32[16,3,4,2048]{3,2,1,0:T(4,128)} async-done(((f32[1,3,4,2048]{3,2,1,0:T(4,128)}), f32[16,3,4,2048]{3,2,1,0:T(4,128)}) %all-gather.13.cloned.1.call-update) | async-done | bytes 1572880 | tf_op jit(solution)/shard_map/all_gather | solution.py:298
  382.0 2.4 reduce_sum.177
  384.3 73.3 %all-gather.11.cloned.1.call-done = bf16[2048,2048]{1,0:T(8,128)(2,1)} async-done(((bf16[128,2048]{1,0:T(8,128)(2,1)}), bf16[2048,2048]{1,0:T(8,128)(2,1)}) %all-gather.11.cloned.1.call-update) | async-done | bytes 8388624 | tf_op jit(solution)/shard_map/all_gather | solution.py:309
  457.6 5.8 %fusion.4 = f32[128,2048]{0,1:T(8,128)S(1)} fusion(bf16[2048,2048]{1,0:T(8,128)(2,1)} %all-gather.11.cloned.1.call-done, bf16[2048,128]{1,0:T(8,128)(2,1)S(1)} %bitcast.263), kind=kOutput, calls=%fused_computation.11 | convolution fusion | flops 1074003968 | bytes 9961472 | tf_op jit(solution)/shard_map/dot_general | solution.py:311
  463.4 1.3 copy.228
  (107 shorter events, 16.3 us)
Async XLA Ops:
  7.2 80.1 %all-gather.7.cloned.1.call-start = ((), (), s32[]{:S(2)}) async-start(), calls=%async_computation.1 | async-start | bytes 8912896 | tf_op jit(solution)/shard_map/all_gather | solution.py:161
  7.9 176.3 %all-gather.15.cloned.1.call-start = ((), (), s32[]{:S(2)}) async-start(), calls=%async_computation.5 | async-start | bytes 9474048 | tf_op jit(solution)/shard_map/all_gather | solution.py:86
  11.9 83.3 %copy-start.21 = (bf16[1,128,2048]{2,1,0:T(8,128)(2,1)S(1)}, bf16[1,128,2048]{2,1,0:T(8,128)(2,1)}, u32[]{:S(2)}) copy-start(bf16[1,128,2048]{2,1,0:T(8,128)(2,1)} %param.12) | copy-start | bytes 1572868
  12.0 83.2 %copy-start.22 = (bf16[1,128,2048]{2,1,0:T(8,128)(2,1)S(1)}, bf16[1,128,2048]{2,1,0:T(8,128)(2,1)}, u32[]{:S(2)}) copy-start(bf16[1,128,2048]{2,1,0:T(8,128)(2,1)} %param.11) | copy-start | bytes 1572868
  92.1 3.1 copy-start.17
  92.1 3.0 collective-permute-start
  97.0 1.8 copy-start.4
  98.8 0.8 copy-start.6
  100.7 192.0 %all-gather.9.cloned.1.call-start = ((), (), s32[]{:S(2)}) async-start(), calls=%async_computation.2 | async-start | bytes 9437184 | tf_op jit(solution)/shard_map/all_gather | solution.py:91
  197.7 2.8 copy-start
  200.4 1.4 copy-start.11
  202.0 5.2 %copy-start.1 = (bf16[128,2048]{0,1:T(8,128)(2,1)S(1)}, bf16[128,2048]{0,1:T(8,128)(2,1)}, u32[]{:S(2)}) copy-start(bf16[128,2048]{0,1:T(8,128)(2,1)} %copy.188) | copy-start | bytes 1572868
  202.0 5.2 %copy-start.13 = (f32[128,16,128]{0,2,1:T(8,128)S(1)}, f32[128,16,128]{0,2,1:T(8,128)}, u32[]{:S(2)}) copy-start(f32[128,16,128]{0,2,1:T(8,128)} %fusion.21) | copy-start | bytes 3145732
  202.0 5.5 %copy-start.7 = (bf16[16,16,8,128]{3,2,1,0:T(8,128)(2,1)S(1)}, bf16[16,16,8,128]{3,2,1,0:T(8,128)(2,1)}, u32[]{:S(2)}) copy-start(bf16[16,16,8,128]{3,2,1,0:T(8,128)(2,1)} %copy-done.6) | copy-start | bytes 1572868
  202.0 5.5 %copy-start.19 = (bf16[16,128,128]{2,1,0:T(8,128)(2,1)S(1)}, bf16[16,128,128]{2,1,0:T(8,128)(2,1)}, u32[]{:S(2)}) copy-start(bf16[16,128,128]{2,1,0:T(8,128)(2,1)} %fusion.22) | copy-start | bytes 1572868
  207.1 1.8 copy-start.8
  207.1 1.6 copy-start.10
  209.9 1.0 copy-start.2
  212.0 169.9 %all-gather.13.cloned.1.call-start = ((), (), s32[]{:S(2)}) async-start(), calls=%async_computation.4 | async-start | bytes 1671168 | tf_op jit(solution)/shard_map/all_gather | solution.py:298
  212.3 3.8 copy-start.3
  212.3 3.8 copy-start.9
  212.3 4.1 copy-start.5
  214.3 3.8 copy-start.18
  321.7 9.0 %collective-permute-start.1 = (bf16[3,3,2048]{2,1,0:T(4,128)(2,1)S(1)}, bf16[3,3,2048]{2,1,0:T(4,128)(2,1)S(1)}, u32[]{:S(2)}, u32[]{:S(2)}) collective-permute-start(bf16[3,3,2048]{2,1,0:T(4,128)(2,1)S(1)} %pad_maximum_fusion.6), channel_id=1, source_target_pairs={{2,0},{4,2},{6,4},{8,6},{10,8},{12,10},{14,12},{3,1},{5,3},{7,5},{... | collective-permute-start | bytes 110600 | tf_op jit(solution)/shard_map/ppermute | solution.py:14
  330.6 4.6 copy-start.15
  335.2 1.8 copy-start.14
  337.0 3.2 copy-start.16
  338.7 24.6 %copy-start.20 = (bf16[128,16,128]{0,2,1:T(8,128)(2,1)S(1)}, bf16[128,16,128]{0,2,1:T(8,128)(2,1)}, u32[]{:S(2)}) copy-start(bf16[128,16,128]{0,2,1:T(8,128)(2,1)} %get-tuple-element.67) | copy-start | bytes 1572868
  338.7 25.6 %copy-start.12 = (bf16[128,2048]{1,0:T(8,128)(2,1)S(1)}, bf16[128,2048]{1,0:T(8,128)(2,1)}, u32[]{:S(2)}) copy-start(bf16[128,2048]{1,0:T(8,128)(2,1)} %get-tuple-element.70) | copy-start | bytes 1572868
  339.6 118.1 %all-gather.11.cloned.1.call-start = ((), (), s32[]{:S(2)}) async-start(), calls=%async_computation.3 | async-start | bytes 8912896 | tf_op jit(solution)/shard_map/all_gather | solution.py:309
Sparse Core Ops, SparseCore 0:
  10.2 76.9 all-gather.6
  100.9 83.2 all-gather.14
  212.1 80.5 all-gather.8
  339.7 42.2 all-gather.12
  384.6 72.9 all-gather.10
